TPU v7x, 128 devices: a whole 4x4x4 slice. The times are simulated.
128 devices in a mesh: seq: 32 (over x, y, core), tp: 4 (over z).
Axes of the slice: x: 4, y: 4, z: 4, core: 2. Of those that a mesh axis runs over, the one named last changes fastest.
Arguments:
- inputs: float32 [8192, 1024], P('seq', 'tp'), may hold values from -6 to 6
- cotangent: float32 [8192, 1024], P('seq', 'tp'), may hold values from -6 to 6
- entry_weight: float32 [2, 3, 1024, 1024], P(None, None, 'seq', 'tp'), may hold values from -0.1875 to 0.1875
- exit_weight: float32 [2, 1024, 1024], P(None, 'tp', 'seq'), may hold values from -0.1875 to 0.1875
- gate_up: float32 [2, 2, 1024, 4608], P(None, None, 'seq', 'tp'), may hold values from -0.1875 to 0.1875
- down_weight: float32 [2, 4608, 1024], P(None, 'tp', 'seq'), may hold values from -0.1875 to 0.1875
- conv_kernel: float32 [2, 3, 1024], P(None, None, 'tp'), may hold values from -3 to 3
- norm_gain: float32 [2, 2, 1024], P(None, None, 'tp'), may hold values from 0.5 to 1.5
- entry_first: float32 [2, 3, 1024, 1024], P(None, None, 'seq', 'tp'), may hold values from -27.1529 to 27.1529
- entry_second: float32 [2, 3, 1024, 1024], P(None, None, 'seq', 'tp'), may hold values from 0.8192 to 16.384
- exit_first: float32 [2, 1024, 1024], P(None, 'tp', 'seq'), may hold values from -27.1529 to 27.1529
- exit_second: float32 [2, 1024, 1024], P(None, 'tp', 'seq'), may hold values from 0.8192 to 16.384
- gate_first: float32 [2, 2, 1024, 4608], P(None, None, 'seq', 'tp'), may hold values from -27.1529 to 27.1529
- gate_second: float32 [2, 2, 1024, 4608], P(None, None, 'seq', 'tp'), may hold values from 0.8192 to 16.384
- down_first: float32 [2, 4608, 1024], P(None, 'tp', 'seq'), may hold values from -27.1529 to 27.1529
- down_second: float32 [2, 4608, 1024], P(None, 'tp', 'seq'), may hold values from 0.8192 to 16.384
- kernel_first: float32 [2, 3, 1024], P(None, None, 'tp'), may hold values from -27.1529 to 27.1529
- kernel_second: float32 [2, 3, 1024], P(None, None, 'tp'), may hold values from 0.8192 to 16.384
- gain_first: float32 [2, 2, 1024], P(None, None, 'tp'), may hold values from -27.1529 to 27.1529
- gain_second: float32 [2, 2, 1024], P(None, None, 'tp'), may hold values from 0.8192 to 16.384
Outputs:
- output: float32 [8192, 1024], P('seq', 'tp')
- input_grad: float32 [8192, 1024], P('seq', 'tp')
- entry_grad: float32 [2, 3, 1024, 1024], P(None, None, 'seq', 'tp')
- exit_grad: float32 [2, 1024, 1024], P(None, 'tp', 'seq')
- gate_grad: float32 [2, 2, 1024, 4608], P(None, None, 'seq', 'tp')
- down_grad: float32 [2, 4608, 1024], P(None, 'tp', 'seq')
- kernel_grad: float32 [2, 3, 1024], P(None, None, 'tp')
- gain_grad: float32 [2, 2, 1024], P(None, None, 'tp')
- entry_updated: float32 [2, 3, 1024, 1024], P(None, None, 'seq', 'tp')
- exit_updated: float32 [2, 1024, 1024], P(None, 'tp', 'seq')
- gate_updated: float32 [2, 2, 1024, 4608], P(None, None, 'seq', 'tp')
- down_updated: float32 [2, 4608, 1024], P(None, 'tp', 'seq')
- kernel_updated: float32 [2, 3, 1024], P(None, None, 'tp')
- gain_updated: float32 [2, 2, 1024], P(None, None, 'tp')
- entry_first_new: float32 [2, 3, 1024, 1024], P(None, None, 'seq', 'tp')
- entry_second_new: float32 [2, 3, 1024, 1024], P(None, None, 'seq', 'tp')
- exit_first_new: float32 [2, 1024, 1024], P(None, 'tp', 'seq')
- exit_second_new: float32 [2, 1024, 1024], P(None, 'tp', 'seq')
- gate_first_new: float32 [2, 2, 1024, 4608], P(None, None, 'seq', 'tp')
- gate_second_new: float32 [2, 2, 1024, 4608], P(None, None, 'seq', 'tp')
- down_first_new: float32 [2, 4608, 1024], P(None, 'tp', 'seq')
- down_second_new: float32 [2, 4608, 1024], P(None, 'tp', 'seq')
- kernel_first_new: float32 [2, 3, 1024], P(None, None, 'tp')
- kernel_second_new: float32 [2, 3, 1024], P(None, None, 'tp')
- gain_first_new: float32 [2, 2, 1024], P(None, None, 'tp')
- gain_second_new: float32 [2, 2, 1024], P(None, None, 'tp')
All inputs are finite; a program needn't handle non-finite values.
Results may differ from a plain program's by a relative error of at most 0.019.
The roundings to bfloat16 on the way count: a program that leaves them out, or rounds other values in their place, can miss the bound.
Values may be sent and summed in bfloat16 or wider, within the bound.
A program may use at most 192 MiB of HBM per device.

v0:
```python
import jax
import jax.numpy as jnp
from jax import lax
from jax.sharding import PartitionSpec as P

STEP = 4


EPS = 1e-06


def from_everyone(value, axis):
    copies = jnp.broadcast_to(value, (lax.axis_size(axis), *value.shape))
    return lax.all_to_all(copies, axis, split_axis=0, concat_axis=0, tiled=True)


def taken_together(value, axis):
    return from_everyone(value, axis).sum(axis=0)


def joined_along(blocks, dim):
    blocks = jnp.moveaxis(blocks, 0, dim)
    dims = blocks.shape
    return blocks.reshape(*dims[:dim], dims[dim] * dims[dim + 1], *dims[dim + 2 :])


def collect(value, axis, dim):
    return joined_along(from_everyone(value, axis), dim)


def cut_along(value, dim, peers):
    dims = value.shape
    blocks = value.reshape(*dims[:dim], peers, dims[dim] // peers, *dims[dim + 1 :])
    return jnp.moveaxis(blocks, dim, 0)


def sent_and_summed(value, axis, dim):
    peers = lax.axis_size(axis)
    blocks = lax.all_to_all(cut_along(value, dim, peers), axis, 0, 0, tiled=True)
    return jnp.sum(blocks, axis=0)


def from_behind(value, axis, by):
    peers = lax.axis_size(axis)
    pairs = [(i, i + by) for i in range(peers) if 0 <= i + by < peers]
    return lax.ppermute(value, axis, pairs)


def gather_turned(arrays, axis, dims):
    turned = [jnp.moveaxis(a, dim, 0) for a, dim in zip(arrays, dims)]
    widths = [t[0].size for t in turned]
    both = jnp.concatenate([t.reshape(-1, w) for t, w in zip(turned, widths)], axis=1)
    out = lax.all_gather(both, axis, axis=0, tiled=True)
    blocks = jnp.split(out, [sum(widths[:k]) for k in range(1, len(widths))], axis=1)
    return tuple(
        (
            jnp.moveaxis(b.reshape(-1, *t.shape[1:]), 0, dim)
            for b, t, dim in zip(blocks, turned, dims)
        )
    )


def packed_total(arrays, axis):
    ravelled, at, done = (jnp.concatenate([a.reshape(-1) for a in arrays]), 0, [])
    running = taken_together(ravelled, axis)
    for a in arrays:
        done.append(running[at : at + a.size].reshape(a.shape))
        at += a.size
    return tuple(done)


def bdot(left, right):
    return jnp.dot(left, right, preferred_element_type=jnp.float32)


def row_norm(value, width):
    sums = taken_together(jnp.sum(value * value, axis=1), "tp")
    scale = lax.rsqrt(sums / width + EPS)[:, None]
    return (value * scale, scale)


def norm_back(dnorm, normed, scale, gain, width):
    dnormed = dnorm * gain
    inner = taken_together(jnp.sum(dnormed * normed, axis=1), "tp")
    return (scale * (dnormed - normed * (inner / width)[:, None]), jnp.sum(dnorm * normed, axis=0))


def whole_rows(shard):
    return collect(shard, "tp", 1)


def whole_grads(shard):
    return collect(shard, "tp", 1)


def channel_sum(partial_value):
    return sent_and_summed(partial_value, "tp", 1)


def adamw(weight, grad, first, second, rate, decay):
    first_new = 0.9 * first + 0.1 * grad
    second_new = 0.999 * second + 0.001 * grad * grad
    update = first_new / (1.0 - 0.9**STEP) / (jnp.sqrt(second_new / (1.0 - 0.999**STEP)) + 1e-08)
    return (weight - rate * (update + decay * weight), first_new, second_new)


def layer_forward(hidden, entry, leave, gates, down, kern, gain, width):
    normed1, scale1 = row_norm(hidden, width)
    first_in = whole_rows((normed1 * gain[0]).astype(jnp.bfloat16))
    projected = jnp.einsum("td,cde->cte", first_in, entry, preferred_element_type=jnp.float32)
    b_part, c_part, x_part = (projected[0], projected[1], projected[2])
    product = b_part * x_part
    before = from_behind(product[-2:], "seq", 1)
    extended = jnp.concatenate([before, product], axis=0)
    conv_out = kern[0] * extended[:-2] + kern[1] * extended[1:-1] + kern[2] * extended[2:]
    gated = (c_part * conv_out).astype(jnp.bfloat16)
    mid = hidden + channel_sum(bdot(gated, leave))
    normed2, scale2 = row_norm(mid, width)
    second_in = whole_rows((normed2 * gain[1]).astype(jnp.bfloat16))
    gate_val = bdot(second_in, gates[0])
    up_val = bdot(second_in, gates[1])
    sig = jax.nn.sigmoid(gate_val)
    swish = gate_val * sig
    acted = (swish * up_val).astype(jnp.bfloat16)
    result = mid + channel_sum(bdot(acted, down))
    kept = (
        normed1,
        scale1,
        first_in,
        b_part,
        c_part,
        x_part,
        extended,
        conv_out,
        gated,
        normed2,
        scale2,
        second_in,
        gate_val,
        up_val,
        sig,
        swish,
        acted,
    )
    return (result, kept)


def layer_backward(grad, kept, entry, leave, gates, down, kern, gain, width):
    (
        normed1,
        scale1,
        first_in,
        b_part,
        c_part,
        x_part,
        extended,
        conv_out,
        gated,
        normed2,
        scale2,
        second_in,
        gate_val,
        up_val,
        sig,
        swish,
        acted,
    ) = kept
    grad_rows = whole_grads(grad.astype(jnp.bfloat16))
    dacted = bdot(grad_rows, down.T)
    down_g = bdot(acted.T, grad_rows)
    dgate = (dacted * up_val * sig * (1.0 + gate_val * (1.0 - sig))).astype(jnp.bfloat16)
    dup = (dacted * swish).astype(jnp.bfloat16)
    gate_g = jnp.stack([bdot(second_in.T, dgate), bdot(second_in.T, dup)])
    dnorm2 = channel_sum(bdot(dgate, gates[0].T) + bdot(dup, gates[1].T))
    back2, dgain2 = norm_back(dnorm2, normed2, scale2, gain[1], width)
    dmid = grad + back2
    mid_rows = whole_grads(dmid.astype(jnp.bfloat16))
    dgated = bdot(mid_rows, leave.T)
    exit_g = bdot(gated.T, mid_rows)
    dc_part = dgated * conv_out
    dconv = dgated * c_part
    kernel_g = jnp.stack(
        [
            jnp.sum(dconv * extended[:-2], axis=0),
            jnp.sum(dconv * extended[1:-1], axis=0),
            jnp.sum(dconv * extended[2:], axis=0),
        ]
    )
    channels = dconv.shape[1]
    zero_one = jnp.zeros((1, channels), jnp.float32)
    zero_two = jnp.zeros((2, channels), jnp.float32)
    dextended = (
        jnp.concatenate([kern[0] * dconv, zero_two], axis=0)
        + jnp.concatenate([zero_one, kern[1] * dconv, zero_one], axis=0)
        + jnp.concatenate([zero_two, kern[2] * dconv], axis=0)
    )
    returned = from_behind(dextended[:2], "seq", -1)
    tokens = dconv.shape[0]
    dproduct = dextended[2:] + jnp.concatenate(
        [jnp.zeros((tokens - 2, channels), jnp.float32), returned], axis=0
    )
    dproj = jnp.stack([dproduct * x_part, dc_part, dproduct * b_part]).astype(jnp.bfloat16)
    entry_g = jnp.einsum("td,cte->cde", first_in, dproj, preferred_element_type=jnp.float32)
    dnorm1 = channel_sum(
        jnp.einsum("cte,cde->td", dproj, entry, preferred_element_type=jnp.float32)
    )
    back1, dgain1 = norm_back(dnorm1, normed1, scale1, gain[0], width)
    return (dmid + back1, (entry_g, exit_g, gate_g, down_g), kernel_g, jnp.stack([dgain1, dgain2]))


def per_device(
    inputs,
    cotangent,
    entry_weight,
    exit_weight,
    gate_up,
    down_weight,
    conv_kernel,
    norm_gain,
    entry_first,
    entry_second,
    exit_first,
    exit_second,
    gate_first,
    gate_second,
    down_first,
    down_second,
    kernel_first,
    kernel_second,
    gain_first,
    gain_second,
):
    width = inputs.shape[1] * lax.axis_size("tp")
    layers = entry_weight.shape[0]
    rounded = (
        entry_weight.astype(jnp.bfloat16),
        exit_weight.astype(jnp.bfloat16),
        gate_up.astype(jnp.bfloat16),
        down_weight.astype(jnp.bfloat16),
    )
    gathered = gather_turned((rounded[0], rounded[1], rounded[2], rounded[3]), "seq", (2, 2, 2, 2))
    hidden = inputs
    kept_all = []
    for layer in range(layers):
        hidden, kept = layer_forward(
            hidden,
            gathered[0][layer],
            gathered[1][layer],
            gathered[2][layer],
            gathered[3][layer],
            conv_kernel[layer],
            norm_gain[layer],
            width,
        )
        kept_all.append(kept)
    grad = cotangent
    matrix_terms = [None] * layers
    kernel_terms = [None] * layers
    gain_terms = [None] * layers
    for layer in reversed(range(layers)):
        grad, terms, kernel_g, gain_g = layer_backward(
            grad,
            kept_all[layer],
            gathered[0][layer],
            gathered[1][layer],
            gathered[2][layer],
            gathered[3][layer],
            conv_kernel[layer],
            norm_gain[layer],
            width,
        )
        matrix_terms[layer] = terms
        kernel_terms[layer] = kernel_g
        gain_terms[layer] = gain_g
    stacked = tuple(
        (jnp.stack([matrix_terms[layer][index] for layer in range(layers)]) for index in range(4))
    )
    summed = lax.psum_scatter(stacked, "seq", scatter_dimension=2, tiled=True)
    kernel_grad, gain_grad = packed_total((jnp.stack(kernel_terms), jnp.stack(gain_terms)), "seq")
    entry_grad, exit_grad, gate_grad, down_grad = summed
    entry_u, entry_f, entry_s = adamw(
        entry_weight, entry_grad, entry_first, entry_second, 0.01, 0.1
    )
    exit_u, exit_f, exit_s = adamw(exit_weight, exit_grad, exit_first, exit_second, 0.01, 0.1)
    gate_u, gate_f, gate_s = adamw(gate_up, gate_grad, gate_first, gate_second, 0.01, 0.1)
    down_u, down_f, down_s = adamw(down_weight, down_grad, down_first, down_second, 0.01, 0.1)
    kernel_u, kernel_f, kernel_s = adamw(
        conv_kernel, kernel_grad, kernel_first, kernel_second, 0.2, 0.0
    )
    gain_u, gain_f, gain_s = adamw(norm_gain, gain_grad, gain_first, gain_second, 0.2, 0.0)
    return (
        hidden,
        grad,
        entry_grad,
        exit_grad,
        gate_grad,
        down_grad,
        kernel_grad,
        gain_grad,
        entry_u,
        exit_u,
        gate_u,
        down_u,
        kernel_u,
        gain_u,
        entry_f,
        entry_s,
        exit_f,
        exit_s,
        gate_f,
        gate_s,
        down_f,
        down_s,
        kernel_f,
        kernel_s,
        gain_f,
        gain_s,
    )


def solution(mesh):
    placed = (
        P("seq", "tp"),
        P("seq", "tp"),
        P(None, None, "seq", "tp"),
        P(None, "tp", "seq"),
        P(None, None, "seq", "tp"),
        P(None, "tp", "seq"),
        P(None, None, "tp"),
        P(None, None, "tp"),
        P(None, None, "seq", "tp"),
        P(None, None, "seq", "tp"),
        P(None, "tp", "seq"),
        P(None, "tp", "seq"),
        P(None, None, "seq", "tp"),
        P(None, None, "seq", "tp"),
        P(None, "tp", "seq"),
        P(None, "tp", "seq"),
        P(None, None, "tp"),
        P(None, None, "tp"),
        P(None, None, "tp"),
        P(None, None, "tp"),
    )
    return jax.shard_map(
        per_device,
        mesh=mesh,
        in_specs=placed,
        out_specs=(
            P("seq", "tp"),
            P("seq", "tp"),
            P(None, None, "seq", "tp"),
            P(None, "tp", "seq"),
            P(None, None, "seq", "tp"),
            P(None, "tp", "seq"),
            P(None, None, "tp"),
            P(None, None, "tp"),
            P(None, None, "seq", "tp"),
            P(None, "tp", "seq"),
            P(None, None, "seq", "tp"),
            P(None, "tp", "seq"),
            P(None, None, "tp"),
            P(None, None, "tp"),
            P(None, None, "seq", "tp"),
            P(None, None, "seq", "tp"),
            P(None, "tp", "seq"),
            P(None, "tp", "seq"),
            P(None, None, "seq", "tp"),
            P(None, None, "seq", "tp"),
            P(None, "tp", "seq"),
            P(None, "tp", "seq"),
            P(None, None, "tp"),
            P(None, None, "tp"),
            P(None, None, "tp"),
            P(None, None, "tp"),
        ),
        check_vma=False,
    )
```

profile of v0, /device:TPU:0, one launch (start us, length us, event | category | flops | bytes accessed | tf_op | source)
XLA Modules:
  0.0 817.0 jit_solution(14901821055226626452)
XLA Ops:
  11.7 5.4 all-to-all-start
  17.2 5.2 all-to-all-done
  26.9 8.2 %all-to-all-done.1 = bf16[4,256,256]{2,1,0:T(8,128)(2,1)S(1)} async-done(((bf16[4,256,256]{2,1,0:T(8,128)(2,1)}), bf16[4,256,256]{2,1,0:T(8,128)(2,1)S(1)}, u32[]{:S(2)}, u32[]{:S(2)}) %all-to-all-start.1) | async-done | bytes 524320 | tf_op jit(solution)/shard_map/all_to_all | solution.py:14
  36.8 52.9 %all-gather.2.cloned.1.call-done = bf16[1024,8960]{1,0:T(8,128)(2,1)} async-done(((bf16[32,8960]{1,0:T(8,128)(2,1)}), bf16[1024,8960]{1,0:T(8,128)(2,1)}) %all-gather.2.cloned.1.call-update) | async-done | bytes 18350096 | tf_op jit(solution)/shard_map/all_gather | solution.py:53
  107.0 20.4 %all_to_all.134 = f32[4,256,256]{2,1,0:T(8,128)S(1)} all-to-all(f32[4,256,256]{2,1,0:T(8,128)S(1)} %convolution_bitcast_fusion.16), channel_id=1, replica_groups=mesh['seq'=32,'tp'=4] {'tp'}, dimensions={0} | all-to-all | bytes 2097152 | tf_op jit(solution)/shard_map/all_to_all | solution.py:39
  131.5 7.9 split.18
  139.4 13.0 %reshape.240 = bf16[1024,2,2,1152]{3,2,1,0:T(2,128)(2,1)} reshape(bf16[1024,4608]{1,0:T(8,128)(2,1)} %split.18) | data formatting | bytes 18874368 | tf_op jit(solution)/shard_map/reshape | solution.py:57
  152.5 8.5 %copy.432 = bf16[1024,2,2,1152]{3,0,2,1:T(8,128)(2,1)} copy(bf16[1024,2,2,1152]{3,2,1,0:T(2,128)(2,1)} %reshape.240) | data formatting | bytes 18874368 | tf_op jit(solution)/shard_map/reshape | solution.py:57
  165.7 6.6 copy.342
  194.8 17.7 %all_to_all.135 = f32[4,256,256]{2,1,0:T(8,128)S(1)} all-to-all(f32[4,256,256]{2,1,0:T(8,128)S(1)} %convolution_bitcast_fusion.15), channel_id=1, replica_groups=mesh['seq'=32,'tp'=4] {'tp'}, dimensions={0} | all-to-all | bytes 2097152 | tf_op jit(solution)/shard_map/all_to_all | solution.py:39
  212.7 7.6 all_to_all.136
  220.5 10.6 %all_to_all.137 = bf16[4,256,256]{2,1,0:T(8,128)(2,1)S(1)} all-to-all(bf16[4,256,256]{2,1,0:T(8,128)(2,1)S(1)} %broadcast_in_dim.64), channel_id=1, replica_groups=mesh['seq'=32,'tp'=4] {'tp'}, dimensions={0} | all-to-all | bytes 1048576 | tf_op jit(solution)/shard_map/all_to_all | solution.py:14
  237.8 18.3 %all_to_all.138 = f32[4,256,256]{2,1,0:T(8,128)S(1)} all-to-all(f32[4,256,256]{2,1,0:T(8,128)S(1)} %convolution_bitcast_fusion.14), channel_id=1, replica_groups=mesh['seq'=32,'tp'=4] {'tp'}, dimensions={0} | all-to-all | bytes 2097152 | tf_op jit(solution)/shard_map/all_to_all | solution.py:39
  256.4 7.7 all_to_all.139
  268.7 9.0 %all-to-all-done.10 = bf16[4,256,256]{1,2,0:T(8,128)(2,1)S(1)} async-done(((bf16[4,256,256]{1,2,0:T(8,128)(2,1)}), bf16[4,256,256]{1,2,0:T(8,128)(2,1)S(1)}, u32[]{:S(2)}, u32[]{:S(2)}) %all-to-all-start.10) | async-done | bytes 524320 | tf_op jit(solution)/shard_map/all_to_all | solution.py:14
  311.2 6.5 all-to-all-done.13
  323.3 9.1 %all-to-all-done.11 = f32[4,256,256]{2,1,0:T(8,128)S(1)} async-done(((f32[4,256,256]{2,1,0:T(8,128)}), f32[4,256,256]{2,1,0:T(8,128)S(1)}, u32[]{:S(2)}, u32[]{:S(2)}) %all-to-all-start.11) | async-done | bytes 1048608 | tf_op jit(solution)/shard_map/all_to_all | solution.py:39
  343.7 10.5 %all_to_all.140 = bf16[4,256,256]{1,2,0:T(8,128)(2,1)S(1)} all-to-all(bf16[4,256,256]{1,2,0:T(8,128)(2,1)S(1)} %broadcast_in_dim.69), channel_id=1, replica_groups=mesh['seq'=32,'tp'=4] {'tp'}, dimensions={0} | all-to-all | bytes 1048576 | tf_op jit(solution)/shard_map/all_to_all | solution.py:14
  361.2 19.6 %all_to_all.141 = f32[4,256,256]{2,1,0:T(8,128)} all-to-all(f32[4,256,256]{2,1,0:T(8,128)S(1)} %convolution_bitcast_fusion.10), channel_id=1, replica_groups=mesh['seq'=32,'tp'=4] {'tp'}, dimensions={0} | all-to-all | bytes 2097152 | tf_op jit(solution)/shard_map/all_to_all | solution.py:39
  382.8 7.6 all_to_all.142
  392.2 11.3 %all_to_all.143 = bf16[4,256,256]{1,2,0:T(8,128)(2,1)S(1)} all-to-all(bf16[4,256,256]{1,2,0:T(8,128)(2,1)S(1)} %broadcast_in_dim.71), channel_id=1, replica_groups=mesh['seq'=32,'tp'=4] {'tp'}, dimensions={0} | all-to-all | bytes 1048576 | tf_op jit(solution)/shard_map/all_to_all | solution.py:14
  426.0 5.6 all-to-all-done.19
  448.1 9.4 %pad_maximum_fusion.1 = f32[2,1152,1024]{2,1,0:T(8,128)} fusion(f32[1,1152,1024]{2,1,0:T(8,128)} %convolution_bitcast_fusion, f32[1,1152,1024]{2,1,0:T(8,128)} %convolution_bitcast_fusion.1), kind=kLoop, calls=%fused_computation.3 | loop fusion | flops 2359296 | bytes 18874368 | tf_op jit(solution)/shard_map/stack | solution.py:276
  457.5 14.9 %copy.367 = f32[2,1152,1024]{1,0,2:T(2,128)} copy(f32[2,1152,1024]{2,1,0:T(8,128)} %pad_maximum_fusion.1) | data formatting | bytes 18874368 | tf_op jit(solution)/shard_map/stack | solution.py:276
  485.8 10.4 %copy.365 = f32[2,3,1024,256]{3,0,1,2:T(2,128)} copy(f32[2,3,1024,256]{2,3,1,0:T(8,128)} %pad_maximum_fusion.2) | data formatting | bytes 12582912 | tf_op jit(solution)/shard_map/stack | solution.py:276
  510.2 6.9 pad_maximum_fusion
  526.4 15.1 %all-to-all-done.22 = f32[4,256,256]{2,1,0:T(8,128)S(1)} async-done(((f32[4,256,256]{2,1,0:T(8,128)}), f32[4,256,256]{2,1,0:T(8,128)S(1)}, u32[]{:S(2)}, u32[]{:S(2)}) %all-to-all-start.22) | async-done | bytes 1048608 | tf_op jit(solution)/shard_map/all_to_all | solution.py:39
  545.8 5.2 all-to-all-done.23
  552.0 5.5 all-to-all-start.24
  558.4 9.8 %all-to-all-done.24 = f32[32,1,2560]{2,1,0:T(1,128)S(1)} async-done(((f32[32,1,2560]{2,1,0:T(1,128)}), f32[32,1,2560]{2,1,0:T(1,128)S(1)}, u32[]{:S(2)}, u32[]{:S(2)}) %all-to-all-start.24) | async-done | bytes 327712 | tf_op jit(solution)/shard_map/all_to_all | solution.py:14
  571.5 109.6 %all-reduce.12.cloned.1.call-done = (f32[2,3,1024,256]{3,0,1,2:T(2,128)}, f32[2,256,1024]{1,0,2:T(2,128)}, f32[2,1152,1024]{1,0,2:T(2,128)}) async-done(((f32[2,3,1024,256]{3,0,1,2:T(2,128)}, f32[2,256,1024]{1,0,2:T(2,128)}, f32[2,1152,1024]{1,0,2:T(2,128)}), (f32[2,3,1024,256]{3,0,1,2:T(2,128)}, f32[2,256,1024]{1,0,2:T(2,128)}, f32[2,1152,1024]{1,0,2:T(2,128)})) %all-reduce.12.cloned.1.call-update) | async-done | bytes 17825808
  686.7 120.7 %reduce-scatter.2.cloned.1.call-done = f32[2,2,32,1152]{3,2,1,0:T(8,128)} async-done(((f32[2,2,1024,1152]{3,2,1,0:T(8,128)}), f32[2,2,32,1152]{3,2,1,0:T(8,128)}) %reduce-scatter.2.cloned.1.call-update) | async-done | bytes 589840 | tf_op jit(solution)/shard_map/reduce_scatter | solution.py:278
  (418 shorter events, 223.5 us)
Async XLA Ops:
  7.2 82.4 %all-gather.2.cloned.1.call-start = ((), (), s32[]{:S(2)}) async-start(), calls=%async_computation.26 | async-start | bytes 18923520 | tf_op jit(solution)/shard_map/all_gather | solution.py:53
  11.7 10.7 %all-to-all-start = ((f32[4,1,256]{2,1,0:T(1,128)}), f32[4,1,256]{2,1,0:T(1,128)S(1)}, u32[]{:S(2)}, u32[]{:S(2)}) async-start(f32[4,1,256]{2,1,0:T(1,128)} %broadcast_in_dim.59), calls=%async_computation | async-start | bytes 8192 | tf_op jit(solution)/shard_map/all_to_all | solution.py:14
  17.1 155.3 %copy-start.78 = (f32[1,1,256]{2,1,0:T(1,128)}, f32[1,1,256]{2,1,0:T(1,128)S(1)}, u32[]{:S(2)}) copy-start(f32[1,1,256]{2,1,0:T(1,128)S(1)} %get-tuple-element.270) | copy-start | bytes 3076
  17.2 364.9 %copy-start.80 = (f32[1,1,256]{2,1,0:T(1,128)}, f32[1,1,256]{2,1,0:T(1,128)S(1)}, u32[]{:S(2)}) copy-start(f32[1,1,256]{2,1,0:T(1,128)S(1)} %get-tuple-element.269) | copy-start | bytes 3076
  23.4 11.8 %all-to-all-start.1 = ((bf16[4,256,256]{2,1,0:T(8,128)(2,1)}), bf16[4,256,256]{2,1,0:T(8,128)(2,1)S(1)}, u32[]{:S(2)}, u32[]{:S(2)}) async-start(bf16[4,256,256]{2,1,0:T(8,128)(2,1)} %broadcast_in_dim.60), calls=%async_computation.1 | async-start | bytes 1048576 | tf_op jit(solution)/shard_map/all_to_all | solution.py:14
  101.3 3.9 collective-permute-start
  128.3 44.1 %all-to-all-start.3 = ((f32[4,1,256]{2,1,0:T(1,128)}), f32[4,1,256]{2,1,0:T(1,128)S(1)}, u32[]{:S(2)}, u32[]{:S(2)}) async-start(f32[4,1,256]{2,1,0:T(1,128)} %broadcast_in_dim.61), calls=%async_computation.3 | async-start | bytes 8192 | tf_op jit(solution)/shard_map/all_to_all | solution.py:14
  173.5 13.9 %all-to-all-start.4 = ((bf16[4,256,256]{1,2,0:T(8,128)(2,1)}), bf16[4,256,256]{1,2,0:T(8,128)(2,1)S(1)}, u32[]{:S(2)}, u32[]{:S(2)}) async-start(bf16[4,256,256]{1,2,0:T(8,128)(2,1)} %broadcast_in_dim.62), calls=%async_computation.4 | async-start | bytes 1048576 | tf_op jit(solution)/shard_map/all_to_all | solution.py:14
  234.2 2.1 collective-permute-start.1
  265.1 12.6 %all-to-all-start.10 = ((bf16[4,256,256]{1,2,0:T(8,128)(2,1)}), bf16[4,256,256]{1,2,0:T(8,128)(2,1)S(1)}, u32[]{:S(2)}, u32[]{:S(2)}) async-start(bf16[4,256,256]{1,2,0:T(8,128)(2,1)} %broadcast_in_dim.66), calls=%async_computation.10 | async-start | bytes 1048576 | tf_op jit(solution)/shard_map/all_to_all | solution.py:14
  278.5 11.5 %all-to-all-start.12 = ((bf16[4,256,256]{1,2,0:T(8,128)(2,1)}), bf16[4,256,256]{1,2,0:T(8,128)(2,1)S(1)}, u32[]{:S(2)}, u32[]{:S(2)}) async-start(bf16[4,256,256]{1,2,0:T(8,128)(2,1)} %broadcast_in_dim.67), calls=%async_computation.12 | async-start | bytes 1048576 | tf_op jit(solution)/shard_map/all_to_all | solution.py:14
  301.0 16.7 %all-to-all-start.13 = ((f32[4,256,256]{2,1,0:T(8,128)}), f32[4,256,256]{2,1,0:T(8,128)}, u32[]{:S(2)}, u32[]{:S(2)}) async-start(f32[4,256,256]{2,1,0:T(8,128)} %bitcast.334), calls=%async_computation.13 | async-start | bytes 2097152 | tf_op jit(solution)/shard_map/all_to_all | solution.py:39
  317.7 14.7 %all-to-all-start.11 = ((f32[4,256,256]{2,1,0:T(8,128)}), f32[4,256,256]{2,1,0:T(8,128)S(1)}, u32[]{:S(2)}, u32[]{:S(2)}) async-start(f32[4,256,256]{2,1,0:T(8,128)} %convolution_bitcast_fusion.13), calls=%async_computation.11 | async-start | bytes 2097152 | tf_op jit(solution)/shard_map/all_to_all | solution.py:39
  333.0 8.5 %all-to-all-start.14 = ((f32[4,1,256]{2,1,0:T(1,128)}), f32[4,1,256]{2,1,0:T(1,128)S(1)}, u32[]{:S(2)}, u32[]{:S(2)}) async-start(f32[4,1,256]{2,1,0:T(1,128)} %broadcast_in_dim.68), calls=%async_computation.14 | async-start | bytes 8192 | tf_op jit(solution)/shard_map/all_to_all | solution.py:14
  356.6 3.2 collective-permute-start.2
  413.9 17.7 %all-to-all-start.19 = ((f32[4,256,256]{2,1,0:T(8,128)}), f32[4,256,256]{2,1,0:T(8,128)}, u32[]{:S(2)}, u32[]{:S(2)}) async-start(f32[4,256,256]{2,1,0:T(8,128)} %bitcast.369), calls=%async_computation.19 | async-start | bytes 2097152 | tf_op jit(solution)/shard_map/all_to_all | solution.py:39
  434.2 8.5 %all-to-all-start.20 = ((f32[4,1,256]{2,1,0:T(1,128)}), f32[4,1,256]{2,1,0:T(1,128)S(1)}, u32[]{:S(2)}, u32[]{:S(2)}) async-start(f32[4,1,256]{2,1,0:T(1,128)} %broadcast_in_dim.72), calls=%async_computation.20 | async-start | bytes 8192 | tf_op jit(solution)/shard_map/all_to_all | solution.py:14
  444.5 27.8 %all-to-all-start.21 = ((bf16[4,256,256]{1,2,0:T(8,128)(2,1)}), bf16[4,256,256]{1,2,0:T(8,128)(2,1)S(1)}, u32[]{:S(2)}, u32[]{:S(2)}) async-start(bf16[4,256,256]{1,2,0:T(8,128)(2,1)} %broadcast_in_dim.73), calls=%async_computation.21 | async-start | bytes 1048576 | tf_op jit(solution)/shard_map/all_to_all | solution.py:14
  448.1 233.0 %all-reduce.12.cloned.1.call-start = ((), (), s32[]{:S(2)}) async-start(), calls=%async_computation.28 | async-start | bytes 35651584
  475.8 3.9 collective-permute-start.3
  496.2 311.3 %reduce-scatter.2.cloned.1.call-start = ((), (), s32[]{:S(2)}) async-start(), calls=%async_computation.27 | async-start | bytes 19464192 | tf_op jit(solution)/shard_map/reduce_scatter | solution.py:278
  520.1 21.4 %all-to-all-start.22 = ((f32[4,256,256]{2,1,0:T(8,128)}), f32[4,256,256]{2,1,0:T(8,128)S(1)}, u32[]{:S(2)}, u32[]{:S(2)}) async-start(f32[4,256,256]{2,1,0:T(8,128)} %convolution_bitcast_fusion.9), calls=%async_computation.22 | async-start | bytes 2097152 | tf_op jit(solution)/shard_map/all_to_all | solution.py:39
  541.6 142.3 %copy-start.65 = (f32[2,256,32]{1,2,0:T(8,128)S(1)}, f32[2,256,32]{1,2,0:T(8,128)}, u32[]{:S(2)}) copy-start(f32[2,256,32]{1,2,0:T(8,128)} %param.23) | copy-start | bytes 196612
  541.6 142.3 %copy-start.68 = (f32[2,256,32]{1,2,0:T(8,128)S(1)}, f32[2,256,32]{1,2,0:T(8,128)}, u32[]{:S(2)}) copy-start(f32[2,256,32]{1,2,0:T(8,128)} %param.30) | copy-start | bytes 196612
  541.6 142.3 %copy-start.69 = (f32[2,256,32]{1,2,0:T(8,128)S(1)}, f32[2,256,32]{1,2,0:T(8,128)}, u32[]{:S(2)}) copy-start(f32[2,256,32]{1,2,0:T(8,128)} %param.31) | copy-start | bytes 196612
  541.7 143.0 %copy-start.49 = (f32[2,3,32,256]{3,2,1,0:T(8,128)S(1)}, f32[2,3,32,256]{3,2,1,0:T(8,128)}, u32[]{:S(2)}) copy-start(f32[2,3,32,256]{3,2,1,0:T(8,128)} %param.22) | copy-start | bytes 589828
  541.7 143.0 %copy-start.66 = (f32[2,3,32,256]{3,2,1,0:T(8,128)S(1)}, f32[2,3,32,256]{3,2,1,0:T(8,128)}, u32[]{:S(2)}) copy-start(f32[2,3,32,256]{3,2,1,0:T(8,128)} %param.28) | copy-start | bytes 589828
  541.7 143.0 %copy-start.67 = (f32[2,3,32,256]{3,2,1,0:T(8,128)S(1)}, f32[2,3,32,256]{3,2,1,0:T(8,128)}, u32[]{:S(2)}) copy-start(f32[2,3,32,256]{3,2,1,0:T(8,128)} %param.29) | copy-start | bytes 589828
  542.5 8.5 %all-to-all-start.23 = ((f32[4,1,256]{2,1,0:T(1,128)}), f32[4,1,256]{2,1,0:T(1,128)S(1)}, u32[]{:S(2)}, u32[]{:S(2)}) async-start(f32[4,1,256]{2,1,0:T(1,128)} %broadcast_in_dim.74), calls=%async_computation.23 | async-start | bytes 8192 | tf_op jit(solution)/shard_map/all_to_all | solution.py:14
  552.0 16.2 %all-to-all-start.24 = ((f32[32,1,2560]{2,1,0:T(1,128)}), f32[32,1,2560]{2,1,0:T(1,128)S(1)}, u32[]{:S(2)}, u32[]{:S(2)}) async-start(f32[32,1,2560]{2,1,0:T(1,128)} %broadcast_in_dim.75), calls=%async_computation.25 | async-start | bytes 655360 | tf_op jit(solution)/shard_map/all_to_all | solution.py:14
  557.5 128.1 %copy-start.37 = (f32[2,1152,32]{1,2,0:T(8,128)S(1)}, f32[2,1152,32]{1,2,0:T(8,128)}, u32[]{:S(2)}) copy-start(f32[2,1152,32]{1,2,0:T(8,128)} %param.25) | copy-start | bytes 884740
  557.6 128.1 %copy-start.62 = (f32[2,1152,32]{1,2,0:T(8,128)S(1)}, f32[2,1152,32]{1,2,0:T(8,128)}, u32[]{:S(2)}) copy-start(f32[2,1152,32]{1,2,0:T(8,128)} %param.34) | copy-start | bytes 884740
  (97 other events, 1976.5 us)
Sparse Core Ops, SparseCore 0:
  11.1 78.4 all-gather.1
  496.3 184.7 all-reduce.11
  685.7 121.7 reduce-scatter.1
where the time goes:
time: 829 us; the launch traced here: 817 us
  waiting for transfers between devices  367 us (44%)
  blocking collectives  131 us (16%)
  local copies, waits for them, and re-layouts  117 us (14%)
  starting transfers between devices  66.1 us (8%)
  matrix products  64.8 us (8%)
  other arithmetic  54.2 us (7%)
  between operations  16.8 us (2%)
    reduce_scatter x1, waiting for transfers between devices, per_device(): summed = lax.psum_scatter(stacked, 'seq', scatter_dimension=2, tiled=True)  121 us
    unnamed x4, waiting for transfers between devices  110 us
    all_to_all x4, blocking collectives, sent_and_summed(): lax.all_to_all(cut_along(value, dim, peers), axis, 0, 0, tiled=True)  76 us
    all_to_all x6, blocking collectives, from_everyone(): return lax.all_to_all(copies, axis, split_axis=0, concat_axis=0, tiled=True)  55.3 us
    dot_general x24, matrix products, bdot(): return jnp.dot(left, right, preferred_element_type=jnp.float32)  54.5 us
    all_gather x1, waiting for transfers between devices, gather_turned(): out = lax.all_gather(both, axis, axis=0, tiled=True)  52.9 us
    all_to_all x11, waiting for transfers between devices, from_everyone(): return lax.all_to_all(copies, axis, split_axis=0, concat_axis=0, tiled=True)  46.2 us
    all_to_all x11, starting transfers between devices, from_everyone(): return lax.all_to_all(copies, axis, split_axis=0, concat_axis=0, tiled=True)  42.6 us
  transfers between devices with their start and end apart: 22, of which 18 were waited for; matrix products, arithmetic and copies ran while one was open for 17% of the time, Pallas kernels for 0%

commit v1 on v0

v1 whole, which is shorter than its diff:
```python
import functools

import jax
import jax.numpy as jnp
from jax import lax
from jax.experimental import pallas as pl
from jax.experimental.pallas import tpu as pltpu
from jax.sharding import PartitionSpec as P

STEP = 4
EPS = 1e-06
MESH = pl.DeviceIdType.MESH
BF = jnp.bfloat16
F32 = jnp.float32
SPAN = 384


def nn(a, b):
    return lax.dot_general(a, b, (((1,), (0,)), ((), ())), preferred_element_type=F32)


def nt(a, b):
    return lax.dot_general(a, b, (((1,), (1,)), ((), ())), preferred_element_type=F32)


def as_column(row):
    return jnp.broadcast_to(row, (128, row.shape[1])).T[:, 0:1]


def step_kernel(
    cfg,
    x_ref,
    cot_ref,
    w_ref,
    kern_ref,
    gain_ref,
    out_ref,
    din_ref,
    gw_ref,
    small_ref,
    rows,
    part,
    stage,
    landed,
    stats,
    normed,
    scales,
    ext,
    dext,
    bcx,
    conv,
    gated,
    gates,
    ups,
    acted,
    dgs,
    dus,
    dproj,
    turned,
    ag_send,
    ag_recv,
    rs_send,
    rs_recv,
    st_send,
    st_recv,
    halo_send,
    halo_recv,
):
    layers, seqs, tokens, ch, ff = cfg
    half = tokens // 2
    width = 4 * ch
    per = 4 * ch + 3 * ff
    z = lax.axis_index("tp")
    s = lax.axis_index("seq")
    zr, zl, zo = lax.rem(z + 1, 4), lax.rem(z + 3, 4), lax.rem(z + 2, 4)
    after, before = lax.rem(s + 1, seqs), lax.rem(s + seqs - 1, seqs)

    barrier = pltpu.get_barrier_semaphore()
    for where in ((s, zr), (s, zl), (s, zo), (after, z), (before, z)):
        pl.semaphore_signal(barrier, inc=1, device_id=where, device_id_type=MESH)
    pl.semaphore_wait(barrier, 5)

    pending = []

    def send(src, dst, ssem, rsem, where):
        copy = pltpu.make_async_remote_copy(
            src_ref=src, dst_ref=dst, send_sem=ssem, recv_sem=rsem, device_id=where, device_id_type=MESH
        )
        copy.start()
        pending.append(copy)
        return copy

    def cols(who):
        return pl.ds(pl.multiple_of(who * ch, ch), ch)

    def own_rows(who):
        return pl.ds(pl.multiple_of(who * ch, ch), ch)

    top, low = pl.ds(0, half), pl.ds(half, half)

    class Gather:
        def __init__(self, i, block):
            self.i = i
            rows[i, :, cols(z)] = block
            mine = lambda r: rows.at[i, r, cols(z)]
            self.r1 = send(mine(top), mine(top), ag_send.at[i, 0], ag_recv.at[i, 0], (s, zr))
            self.l1 = send(mine(low), mine(low), ag_send.at[i, 1], ag_recv.at[i, 1], (s, zl))
            self.r2 = send(mine(low), mine(low), ag_send.at[i, 2], ag_recv.at[i, 2], (s, zr))
            self.l2 = send(mine(top), mine(top), ag_send.at[i, 3], ag_recv.at[i, 3], (s, zl))

        def pass_on(self):
            i = self.i
            self.r1.wait_recv()
            b = rows.at[i, top, cols(zl)]
            self.rf = send(b, b, ag_send.at[i, 4], ag_recv.at[i, 4], (s, zr))
            self.l1.wait_recv()
            b = rows.at[i, low, cols(zr)]
            self.lf = send(b, b, ag_send.at[i, 5], ag_recv.at[i, 5], (s, zl))

        def finish(self):
            for c in (self.r2, self.l2, self.rf, self.lf):
                c.wait_recv()

    class Scatter:
        def __init__(self, i, piece):
            self.i = i
            at = lambda k, r: stage.at[i, k, r]
            to = lambda k: landed.at[i, k]
            stage[i, 0] = piece(zo).astype(BF)
            self.r1 = send(at(0, top), to(0), rs_send.at[i, 0], rs_recv.at[i, 0], (s, zr))
            self.l1 = send(at(0, low), to(1), rs_send.at[i, 1], rs_recv.at[i, 1], (s, zl))
            right = piece(zr)
            stage[i, 1, half:] = right[half:].astype(BF)
            self.r2 = send(at(1, low), to(2), rs_send.at[i, 2], rs_recv.at[i, 2], (s, zr))
            part[0] = right[:half]
            left = piece(zl)
            stage[i, 2, :half] = left[:half].astype(BF)
            self.l2 = send(at(2, top), to(3), rs_send.at[i, 3], rs_recv.at[i, 3], (s, zl))
            part[1] = left[half:]
            own = piece(z)
            part[2] = own[:half]
            part[3] = own[half:]

        def pass_on(self):
            i = self.i
            self.r1.wait_recv()
            stage[i, 1, :half] = (part[0] + landed[i, 0].astype(F32)).astype(BF)
            self.rf = send(stage.at[i, 1, top], landed.at[i, 4], rs_send.at[i, 4], rs_recv.at[i, 4], (s, zr))
            self.l1.wait_recv()
            stage[i, 2, half:] = (part[1] + landed[i, 1].astype(F32)).astype(BF)
            self.lf = send(stage.at[i, 2, low], landed.at[i, 5], rs_send.at[i, 5], rs_recv.at[i, 5], (s, zl))

        def finish(self):
            i = self.i
            for c in (self.r2, self.l2, self.rf, self.lf):
                c.wait_recv()
            upper = part[2] + landed[i, 4].astype(F32) + landed[i, 3].astype(F32)
            lower = part[3] + landed[i, 2].astype(F32) + landed[i, 5].astype(F32)
            return jnp.concatenate([upper, lower], axis=0)

    def row_total(i, value):
        sums = jnp.sum(value, axis=1, keepdims=True)
        stats[i, z] = jnp.broadcast_to(sums, (tokens, 128)).T[0:8]
        there = stats.at[i, z]
        got = [
            send(there, there, st_send.at[i, k], st_recv.at[i, k], (s, who))
            for k, who in enumerate((zr, zl, zo))
        ]
        for c in got:
            c.wait_recv()
        total = stats[i, 0] + stats[i, 1] + stats[i, 2] + stats[i, 3]
        return as_column(total[0:1])

    def columns(at, j, size=SPAN):
        return pl.ds(pl.multiple_of(at + j * size, 128), size)

    def weight_grad(left_index, spans):
        turned[...] = rows[left_index].T
        for right_ref, lead, width_r, at in spans:
            size = SPAN if width_r % SPAN == 0 else width_r

            @pl.loop(0, width_r // size)
            def _(j, right_ref=right_ref, lead=lead, at=at, size=size):
                right = right_ref[lead, :, columns(0, j, size)]
                gw_ref[:, columns(at, j, size)] = nn(turned[...], right).astype(BF)

    def norm_forward(k, h, gain):
        total = row_total(k, h * h)
        scale = lax.rsqrt(total / width + EPS)
        scales[k] = jnp.broadcast_to(scale, (tokens, 128))
        a = h * scale
        normed[k] = a
        return (a * gain).astype(BF)

    def norm_backward(k, dn, gain, small_row):
        a = normed[k]
        t = dn * gain
        small_ref[pl.ds(small_row, 1), :] = jnp.sum(dn * a, axis=0, keepdims=True)
        inner = row_total(2 * layers + k, t * a)
        return scales[k][:, 0:1] * (t - a * (inner / width))

    small_ref[...] = jnp.zeros_like(small_ref)
    hidden = x_ref[...]
    cot_gather = None
    for l in range(layers):
        base = l * per
        at_exit, at_gate, at_up, at_down = base + 3 * ch, base + 4 * ch, base + 4 * ch + ff, base + 4 * ch + 2 * ff
        n1 = norm_forward(2 * l, hidden, gain_ref[l, 0:1])
        gather = Gather(2 * l, n1)
        if l == 0:
            cot_gather = Gather(2 * layers + 2 * (layers - 1), cot_ref[...].astype(BF))
        gather.pass_on()
        gather.finish()
        if l == 0:
            cot_gather.pass_on()
        full = rows[2 * l]
        bm = nn(full, w_ref[:, columns(base, 0, ch)])
        xm = nn(full, w_ref[:, columns(base, 2, ch)])
        bx = bm * xm
        ext[l, 8:] = bx
        tail = send(
            ext.at[l, pl.ds(tokens, 8)], ext.at[l, pl.ds(0, 8)], halo_send.at[l], halo_recv.at[l], (after, z)
        )
        bcx[l, 0] = bm
        bcx[l, 2] = xm
        cm = nn(full, w_ref[:, columns(base, 1, ch)])
        bcx[l, 1] = cm
        tail.wait_recv()
        head = ext[l, 0:8]
        ext[l, 0:8] = jnp.where(s > 0, head, jnp.zeros_like(head))
        k = kern_ref[l]
        zc = k[0:1] * ext[l, 6 : 6 + tokens] + k[1:2] * ext[l, 7 : 7 + tokens] + k[2:3] * ext[l, 8 : 8 + tokens]
        conv[l] = zc
        gated[l] = (cm * zc).astype(BF)

        def exit_piece(who, l=l, at=at_exit):
            return nt(gated[l], w_ref[own_rows(who), columns(at, 0, ch)])

        scatter = Scatter(2 * l, exit_piece)
        scatter.pass_on()
        mid = hidden + scatter.finish()
        n2 = norm_forward(2 * l + 1, mid, gain_ref[l, 1:2])
        gather = Gather(2 * l + 1, n2)
        gather.pass_on()
        gather.finish()

        @pl.loop(0, ff // SPAN)
        def _(j, l=l, at_gate=at_gate, at_up=at_up):
            full = rows[2 * l + 1]
            g = nn(full, w_ref[:, columns(at_gate, j)])
            u = nn(full, w_ref[:, columns(at_up, j)])
            gates[l, :, columns(0, j)] = g
            ups[l, :, columns(0, j)] = u
            acted[l, :, columns(0, j)] = (g * jax.nn.sigmoid(g) * u).astype(BF)

        def down_piece(who, l=l, at=at_down):
            return nt(acted[l], w_ref[own_rows(who), columns(at, 0, ff)])

        scatter = Scatter(2 * l + 1, down_piece)
        scatter.pass_on()
        hidden = mid + scatter.finish()
    out_ref[...] = hidden

    grad = cot_ref[...]
    for l in reversed(range(layers)):
        base = l * per
        at_exit, at_gate, at_up, at_down = base + 3 * ch, base + 4 * ch, base + 4 * ch + ff, base + 4 * ch + 2 * ff
        ie = 2 * layers + 2 * l
        if l == layers - 1:
            gather = cot_gather
        else:
            gather = Gather(ie, grad.astype(BF))
            gather.pass_on()
        gather.finish()

        @pl.loop(0, ff // SPAN)
        def _(j, l=l, ie=ie, at_down=at_down):
            ds = nn(rows[ie], w_ref[:, columns(at_down, j)])
            g = gates[l, :, columns(0, j)]
            u = ups[l, :, columns(0, j)]
            sig = jax.nn.sigmoid(g)
            dgs[0, :, columns(0, j)] = (ds * u * sig * (1.0 + g * (1.0 - sig))).astype(BF)
            dus[0, :, columns(0, j)] = (ds * (g * sig)).astype(BF)

        def norm2_piece(who, at_gate=at_gate, at_up=at_up):
            return nt(dgs[0], w_ref[own_rows(who), columns(at_gate, 0, ff)]) + nt(
                dus[0], w_ref[own_rows(who), columns(at_up, 0, ff)]
            )

        scatter = Scatter(2 * layers + 2 * l, norm2_piece)
        weight_grad(ie, [(acted, l, ff, at_down)])
        scatter.pass_on()
        weight_grad(2 * l + 1, [(dgs, 0, ff, at_gate), (dus, 0, ff, at_up)])
        dn2 = scatter.finish()
        dmid = grad + norm_backward(2 * l + 1, dn2, gain_ref[l, 1:2], 3 * layers + 2 * l + 1)
        gather = Gather(ie + 1, dmid.astype(BF))
        gather.pass_on()
        gather.finish()
        dy = nn(rows[ie + 1], w_ref[:, columns(at_exit, 0, ch)])
        dz = dy * bcx[l, 1]
        dext[l, :tokens] = dz
        tail = send(
            dext.at[l, pl.ds(0, 8)],
            dext.at[l, pl.ds(tokens, 8)],
            halo_send.at[layers + l],
            halo_recv.at[layers + l],
            (before, z),
        )
        dproj[0, :, ch : 2 * ch] = (dy * conv[l]).astype(BF)
        for j in range(3):
            small_ref[pl.ds(3 * l + j, 1), :] = jnp.sum(dz * ext[l, 6 + j : 6 + j + tokens], axis=0, keepdims=True)
        weight_grad(ie + 1, [(gated, l, ch, at_exit)])
        tail.wait_recv()
        last = dext[l, tokens:]
        dext[l, tokens:] = jnp.where(s < seqs - 1, last, jnp.zeros_like(last))
        k = kern_ref[l]
        dbx = k[2:3] * dext[l, 0:tokens] + k[1:2] * dext[l, 1 : 1 + tokens] + k[0:1] * dext[l, 2 : 2 + tokens]
        dproj[0, :, :ch] = (dbx * bcx[l, 2]).astype(BF)
        dproj[0, :, 2 * ch :] = (dbx * bcx[l, 0]).astype(BF)

        def norm1_piece(who, base=base):
            return nt(dproj[0], w_ref[own_rows(who), columns(base, 0, 3 * ch)])

        scatter = Scatter(2 * layers + 2 * l + 1, norm1_piece)
        scatter.pass_on()
        weight_grad(2 * l, [(dproj, 0, 3 * ch, base)])
        dn1 = scatter.finish()
        grad = dmid + norm_backward(2 * l, dn1, gain_ref[l, 0:1], 3 * layers + 2 * l)
    din_ref[...] = grad
    for copy in pending:
        copy.wait_send()


def run_step(x, cot, w, kern, gain, seqs):
    layers, taps, ch = kern.shape
    tokens = x.shape[0]
    width = w.shape[0]
    per = w.shape[1] // layers
    ff = (per - 4 * ch) // 3
    n = 4 * layers
    vmem = pl.BlockSpec(memory_space=pltpu.VMEM)
    dma = pltpu.SemaphoreType.DMA
    return pl.pallas_call(
        functools.partial(step_kernel, (layers, seqs, tokens, ch, ff)),
        out_shape=(
            jax.ShapeDtypeStruct((tokens, ch), F32),
            jax.ShapeDtypeStruct((tokens, ch), F32),
            jax.ShapeDtypeStruct(w.shape, BF),
            jax.ShapeDtypeStruct((16, ch), F32),
        ),
        in_specs=[vmem] * 5,
        out_specs=(vmem,) * 4,
        scratch_shapes=[
            pltpu.VMEM((n, tokens, width), BF),
            pltpu.VMEM((4, tokens // 2, ch), F32),
            pltpu.VMEM((n, 3, tokens, ch), BF),
            pltpu.VMEM((n, 6, tokens // 2, ch), BF),
            pltpu.VMEM((n, 4, 8, tokens), F32),
            pltpu.VMEM((2 * layers, tokens, ch), F32),
            pltpu.VMEM((2 * layers, tokens, 128), F32),
            pltpu.VMEM((layers, tokens + 8, ch), F32),
            pltpu.VMEM((layers, tokens + 8, ch), F32),
            pltpu.VMEM((layers, 3, tokens, ch), F32),
            pltpu.VMEM((layers, tokens, ch), F32),
            pltpu.VMEM((layers, tokens, ch), BF),
            pltpu.VMEM((layers, tokens, ff), F32),
            pltpu.VMEM((layers, tokens, ff), F32),
            pltpu.VMEM((layers, tokens, ff), BF),
            pltpu.VMEM((1, tokens, ff), BF),
            pltpu.VMEM((1, tokens, ff), BF),
            pltpu.VMEM((1, tokens, 3 * ch), BF),
            pltpu.VMEM((width, tokens), BF),
            dma((n, 6)),
            dma((n, 6)),
            dma((n, 6)),
            dma((n, 6)),
            dma((n, 3)),
            dma((n, 3)),
            dma((2 * layers,)),
            dma((2 * layers,)),
        ],
        compiler_params=pltpu.CompilerParams(
            collective_id=0, has_side_effects=True, vmem_limit_bytes=62 * 1024 * 1024
        ),
        name="layers",
    )(x, cot, w, kern, gain)


def adamw(weight, grad, first, second, rate, decay):
    first_new = 0.9 * first + 0.1 * grad
    second_new = 0.999 * second + 0.001 * grad * grad
    update = first_new / (1.0 - 0.9**STEP) / (jnp.sqrt(second_new / (1.0 - 0.999**STEP)) + 1e-08)
    return (weight - rate * (update + decay * weight), first_new, second_new)


def laid_out(entry, leave, gates, down):
    layers = entry.shape[0]
    parts = []
    for l in range(layers):
        parts += [entry[l, 0], entry[l, 1], entry[l, 2], leave[l].T, gates[l, 0], gates[l, 1], down[l].T]
    return jnp.concatenate(parts, axis=1)


def taken_apart(flat, layers, ch, ff):
    per = 4 * ch + 3 * ff
    entry, leave, gates, down = [], [], [], []
    for l in range(layers):
        b = l * per
        entry.append(jnp.stack([flat[:, b + c * ch : b + (c + 1) * ch] for c in range(3)]))
        leave.append(flat[:, b + 3 * ch : b + 4 * ch].T)
        g = b + 4 * ch
        gates.append(jnp.stack([flat[:, g : g + ff], flat[:, g + ff : g + 2 * ff]]))
        down.append(flat[:, g + 2 * ff : g + 3 * ff].T)
    return tuple(jnp.stack(v) for v in (entry, leave, gates, down))


def per_device(
    inputs,
    cotangent,
    entry_weight,
    exit_weight,
    gate_up,
    down_weight,
    conv_kernel,
    norm_gain,
    entry_first,
    entry_second,
    exit_first,
    exit_second,
    gate_first,
    gate_second,
    down_first,
    down_second,
    kernel_first,
    kernel_second,
    gain_first,
    gain_second,
):
    layers, _, _, ch = entry_weight.shape
    ff = gate_up.shape[3]
    seqs = lax.axis_size("seq")
    mine = laid_out(
        entry_weight.astype(BF), exit_weight.astype(BF), gate_up.astype(BF), down_weight.astype(BF)
    )
    whole = lax.all_gather(mine, "seq", axis=0, tiled=True)
    hidden, grad, terms, small = run_step(inputs, cotangent, whole, conv_kernel, norm_gain, seqs)
    summed = lax.psum_scatter(terms, "seq", scatter_dimension=0, tiled=True).astype(F32)
    small = lax.psum(small, "seq")
    entry_grad, exit_grad, gate_grad, down_grad = taken_apart(summed, layers, ch, ff)
    kernel_grad = small[: 3 * layers].reshape(layers, 3, ch)
    gain_grad = small[3 * layers : 5 * layers].reshape(layers, 2, ch)
    entry_u, entry_f, entry_s = adamw(entry_weight, entry_grad, entry_first, entry_second, 0.01, 0.1)
    exit_u, exit_f, exit_s = adamw(exit_weight, exit_grad, exit_first, exit_second, 0.01, 0.1)
    gate_u, gate_f, gate_s = adamw(gate_up, gate_grad, gate_first, gate_second, 0.01, 0.1)
    down_u, down_f, down_s = adamw(down_weight, down_grad, down_first, down_second, 0.01, 0.1)
    kernel_u, kernel_f, kernel_s = adamw(conv_kernel, kernel_grad, kernel_first, kernel_second, 0.2, 0.0)
    gain_u, gain_f, gain_s = adamw(norm_gain, gain_grad, gain_first, gain_second, 0.2, 0.0)
    return (
        hidden,
        grad,
        entry_grad,
        exit_grad,
        gate_grad,
        down_grad,
        kernel_grad,
        gain_grad,
        entry_u,
        exit_u,
        gate_u,
        down_u,
        kernel_u,
        gain_u,
        entry_f,
        entry_s,
        exit_f,
        exit_s,
        gate_f,
        gate_s,
        down_f,
        down_s,
        kernel_f,
        kernel_s,
        gain_f,
        gain_s,
    )


def solution(mesh):
    tokens, rows, columns, replicated = (
        P("seq", "tp"),
        P(None, None, "seq", "tp"),
        P(None, "tp", "seq"),
        P(None, None, "tp"),
    )
    matrices = (rows, columns, rows, columns)
    moments = (rows, rows, columns, columns, rows, rows, columns, columns)
    return jax.shard_map(
        per_device,
        mesh=mesh,
        in_specs=(tokens, tokens, *matrices, replicated, replicated, *moments, *([replicated] * 4)),
        out_specs=(
            tokens,
            tokens,
            *matrices,
            replicated,
            replicated,
            *matrices,
            replicated,
            replicated,
            *moments,
            *([replicated] * 4),
        ),
        check_vma=False,
    )
```

time: 829 us -> 426 us (0.51); the launches traced: 817 us -> 425 us
  waiting for transfers between devices: 367 us -> 78 us
  Pallas kernels: 0 us -> 188 us
  local copies, waits for them, and re-layouts: 117 us -> 7.9 us
  starting transfers between devices: 66.1 us -> 0.08 us
  matrix products: 64.8 us -> 0 us
  other arithmetic: 54.2 us -> 8.91 us
    pallas_call x0 -> x1, Pallas kernels: none -> 188 us  [run_step(): pl.pallas_call(functools.partial(step_kernel, (layers, seqs, tokens, ch,...]
    all_to_all x10 -> x0, blocking collectives: 131 us -> none  [the longest x4 76 us: sent_and_summed(): lax.all_to_all(cut_along(value, dim, peers), axis, 0, 0, tiled=True)]
    psum x0 -> x1, blocking collectives: none -> 128 us  [per_device(): small = lax.psum(small, 'seq')]
    reduce_scatter x1, waiting for transfers between devices: 121 us -> 0.01 us  [per_device(): lax.psum_scatter(terms, 'seq', scatter_dimension=0, tiled=True).astype(F32)]
    unnamed x4 -> x2, waiting for transfers between devices: 110 us -> 0.03 us
    all_to_all x15 -> x0, waiting for transfers between devices: 82.4 us -> none  [the longest x11 46.2 us: from_everyone(): return lax.all_to_all(copies, axis, split_axis=0, concat_axis=0, tiled=True)]
    dot_general x30 -> x0, matrix products: 64.8 us -> none  [the longest x24 54.5 us: bdot(): return jnp.dot(left, right, preferred_element_type=jnp.float32)]
    all_to_all x15 -> x0, starting transfers between devices: 59.6 us -> none  [the longest x11 42.6 us: from_everyone(): return lax.all_to_all(copies, axis, split_axis=0, concat_axis=0, tiled=True)]
  transfers between devices with their start and end apart: 22 -> 2, of which waited for: 18 -> 1; matrix products, arithmetic and copies ran while one was open for 17% -> 1% of each run, Pallas kernels for 0% -> 0%
where the time goes in v1:
time: 426 us; the launch traced here: 425 us
  Pallas kernels  188 us (44%)
  blocking collectives  128 us (30%)
  waiting for transfers between devices  78 us (18%)
  between operations  14.4 us (3%)
  other arithmetic  8.91 us (2%)
  local copies, waits for them, and re-layouts  7.9 us (2%)
    pallas_call x1, Pallas kernels, run_step(): pl.pallas_call(functools.partial(step_kernel, (layers, seqs, tokens, ch,...  188 us
    psum x1, blocking collectives, per_device(): small = lax.psum(small, 'seq')  128 us
    all_gather x1, waiting for transfers between devices, per_device(): whole = lax.all_gather(mine, 'seq', axis=0, tiled=True)  78 us
  transfers between devices with their start and end apart: 2, of which 1 were waited for; matrix products, arithmetic and copies ran while one was open for 1% of the time, Pallas kernels for 0%

profile of v1, /device:TPU:0, one launch (start us, length us, event | category | flops | bytes accessed | tf_op | source)
XLA Modules:
  0.0 425.3 jit_solution(10315374480895745897)
XLA Ops:
  7.2 0.0 all-gather.2.cloned.1.call-start
  7.3 0.9 convert_element_type.16
  8.2 0.9 convert_element_type.15
  9.1 1.0 convert_element_type.18
  10.4 0.8 copy-done.3
  11.2 0.0 reduce-scatter.2.cloned.1.call-start
  11.2 0.6 copy.51.kern_ref
  11.8 78.0 %all-gather.2.cloned.1.call-done.w_ref = bf16[1024,8960]{1,0:T(8,128)(2,1)} async-done(((bf16[32,8960]{1,0:T(8,128)(2,1)}), bf16[1024,8960]{1,0:T(8,128)(2,1)}) %all-gather.2.cloned.1.call-update) | async-done | bytes 18350096 | tf_op jit(solution)/shard_map/all_gather | solution.py:445
  89.8 187.6 %layers.1 = (f32[256,256]{1,0:T(8,128)}, f32[256,256]{1,0:T(8,128)}, bf16[1024,8960]{1,0:T(8,128)(2,1)}, f32[16,256]{1,0:T(8,128)}) custom-call(f32[256,256]{1,0:T(8,128)} %x_ref.1, f32[256,256]{1,0:T(8,128)} %cot_ref.1, bf16[1024,8960]{1,0:T(8,128)(2,1)} %all-gather.2.cloned.1.call-done.w_ref, f32[2,3,256]{2,1,0:T(4,128)} %copy.51.kern_ref, ...), custom_call_target="tpu_custom_call" | custom-call | tf_op jit(solution)/shard_map/layers/pallas_call | solution.py:343
  277.5 0.0 reduce-scatter.2.cloned.1.call-update
  277.5 0.6 copy-done.18
  278.1 128.4 %psum.7 = f32[16,256]{1,0:T(8,128)S(1)} all-reduce(f32[16,256]{1,0:T(8,128)S(1)} %copy-done.18), channel_id=1, replica_groups=mesh['seq'=32,'tp'=4] {'seq'}, use_global_device_ids=true, to_apply=%region_1.0 | all-reduce | flops 4096 | bytes 32768 | tf_op jit(solution)/shard_map/psum | solution.py:448
  406.5 0.6 copy.56
  407.2 0.6 copy.57
  407.8 0.6 copy.58
  408.4 0.6 copy.59
  409.0 0.6 multiply_subtract_fusion.5
  409.6 1.1 convert_element_type.19
  410.8 0.1 slice_bitcast_fusion.1
  410.9 0.7 copy-done.10
  411.6 0.0 copy-done.13
  411.6 0.0 copy-done.14
  411.6 0.7 multiply_subtract_fusion.3
  412.4 0.9 multiply_subtract_fusion.2
  413.4 0.2 copy-done.6
  413.6 0.2 copy-done.7
  413.8 1.1 multiply_subtract_fusion.1
  414.9 0.2 copy-done.4
  415.1 0.4 copy-done.5
  415.5 1.5 multiply_subtract_fusion
  417.0 0.7 copy.84
  417.7 0.7 copy.85
  (62 shorter events, 0.4 us)
Async XLA Ops:
  7.2 2.9 copy-start
  7.2 82.6 %all-gather.2.cloned.1.call-start = ((), (), s32[]{:S(2)}) async-start(), calls=%async_computation.1 | async-start | bytes 18923520 | tf_op jit(solution)/shard_map/all_gather | solution.py:445
  10.1 1.1 copy-start.15
  10.3 0.8 copy-start.3
  11.2 398.4 %reduce-scatter.2.cloned.1.call-start = ((), (), s32[]{:S(2)}) async-start(), calls=%async_computation.2 | async-start | bytes 18923520 | tf_op jit(solution)/shard_map/reduce_scatter | solution.py:447
  277.4 0.7 copy-start.18
  277.4 129.7 %copy-start.19 = (f32[2,3,256]{2,0,1:T(2,128)S(1)}, f32[2,3,256]{2,0,1:T(2,128)}, u32[]{:S(2)}) copy-start(f32[2,3,256]{2,0,1:T(2,128)} %param.36) | copy-start | bytes 18436
  277.4 129.7 %copy-start.20 = (f32[2,3,256]{2,0,1:T(2,128)S(1)}, f32[2,3,256]{2,0,1:T(2,128)}, u32[]{:S(2)}) copy-start(f32[2,3,256]{2,0,1:T(2,128)} %param.37) | copy-start | bytes 18436
  277.4 131.5 %copy-start.16 = (f32[2,2,256]{2,1,0:T(2,128)S(1)}, f32[2,2,256]{2,1,0:T(2,128)}, u32[]{:S(2)}) copy-start(f32[2,2,256]{2,1,0:T(2,128)} %gain_ref.1) | copy-start | bytes 12292
  277.4 131.5 %copy-start.21 = (f32[2,2,256]{2,1,0:T(2,128)S(1)}, f32[2,2,256]{2,1,0:T(2,128)}, u32[]{:S(2)}) copy-start(f32[2,2,256]{2,1,0:T(2,128)} %param.38) | copy-start | bytes 12292
  277.5 131.5 %copy-start.22 = (f32[2,2,256]{2,1,0:T(2,128)S(1)}, f32[2,2,256]{2,1,0:T(2,128)}, u32[]{:S(2)}) copy-start(f32[2,2,256]{2,1,0:T(2,128)} %param.39) | copy-start | bytes 12292
  406.5 4.3 %copy-start.17 = (f32[2,2,256]{2,1,0:T(2,128)}, f32[2,2,256]{2,1,0:T(2,128)S(1)}, u32[]{:S(2)}) copy-start(f32[2,2,256]{2,1,0:T(2,128)S(1)} %reshape.59) | copy-start | bytes 12292
  410.7 0.8 copy-start.10
  410.7 0.9 copy-start.13
  410.8 0.9 copy-start.14
  410.8 1.6 copy-start.2
  410.8 1.6 copy-start.11
  410.8 1.6 copy-start.12
  412.4 1.0 copy-start.1
  412.4 1.2 copy-start.6
  412.4 1.4 copy-start.7
  413.8 1.3 copy-start.4
  413.8 1.7 copy-start.5
  415.5 1.5 copy-start.9
  415.5 2.2 copy-start.8
Sparse Core Ops, SparseCore 0:
  11.3 78.4 all-gather.1
  277.6 117.7 reduce-scatter.1

commit v2 on v1

--- a/solution.py
+++ b/solution.py
@@ -31,12 +31,12 @@
     cfg,
     x_ref,
     cot_ref,
-    w_ref,
+    mine_ref,
     kern_ref,
     gain_ref,
     out_ref,
     din_ref,
-    gw_ref,
+    final_ref,
     small_ref,
     rows,
     part,
@@ -51,12 +51,16 @@
     conv,
     gated,
     gates,
-    ups,
     acted,
-    dgs,
-    dus,
+    dgates,
     dproj,
     turned,
+    w_ref,
+    gw_ref,
+    from_pair,
+    from_far,
+    from_near,
+    tally,
     ag_send,
     ag_recv,
     rs_send,
@@ -65,6 +69,13 @@
     st_recv,
     halo_send,
     halo_recv,
+    w_send,
+    w_recv,
+    g_send,
+    g_recv,
+    t_send,
+    t_recv,
+    credit,
 ):
     layers, seqs, tokens, ch, ff = cfg
     half = tokens // 2
@@ -75,10 +86,28 @@
     zr, zl, zo = lax.rem(z + 1, 4), lax.rem(z + 3, 4), lax.rem(z + 2, 4)
     after, before = lax.rem(s + 1, seqs), lax.rem(s + seqs - 1, seqs)
 
+    c = lax.rem(s, 2)
+    x, y = lax.div(s, 8), lax.rem(lax.div(s, 2), 4)
+    u, v = x * (1 - c) + y * c, y * (1 - c) + x * c
+
+    def place(uu, vv):
+        return uu * (1 - c) + vv * c, vv * (1 - c) + uu * c
+
+    def device(uu, vv):
+        px, py = place(uu, vv)
+        return (px * 8 + py * 2 + c, z)
+
+    up, un, uo = lax.rem(u + 3, 4), lax.rem(u + 1, 4), lax.rem(u + 2, 4)
+    vp, vn, vo = lax.rem(v + 3, 4), lax.rem(v + 1, 4), lax.rem(v + 2, 4)
+    u_next, u_prev, v_next, v_prev = device(un, v), device(up, v), device(u, vn), device(u, vp)
+    pair = (s + 1 - 2 * c, z)
+
     barrier = pltpu.get_barrier_semaphore()
-    for where in ((s, zr), (s, zl), (s, zo), (after, z), (before, z)):
+    partners = [(s, zr), (s, zl), (s, zo), (after, z), (before, z), u_next, u_prev, v_next, v_prev, pair]
+    partners += [device(uo, v), device(u, vo)]
+    for where in partners:
         pl.semaphore_signal(barrier, inc=1, device_id=where, device_id_type=MESH)
-    pl.semaphore_wait(barrier, 5)
+    pl.semaphore_wait(barrier, len(partners))
 
     pending = []
 
@@ -97,6 +126,237 @@
         return pl.ds(pl.multiple_of(who * ch, ch), ch)
 
     top, low = pl.ds(0, half), pl.ds(half, half)
+
+    def chunk_of(ref, lead, vv, lo, hi, where):
+        if lead == 0:
+            return ref.at[pl.ds(lo, hi - lo), vv, 0, :, where]
+        return ref.at[vv, pl.ds(lo, hi - lo), 1, :, where]
+
+    def send_either(make, ssem, rsem, where, held=pending):
+        for core in (0, 1):
+
+            @pl.when(c == core)
+            def _(core=core):
+                src, dst = make(core)
+                pltpu.make_async_remote_copy(
+                    src_ref=src, dst_ref=dst, send_sem=ssem, recv_sem=rsem, device_id=where, device_id_type=MESH
+                ).start()
+
+        src, dst = make(0)
+        copy = pltpu.make_async_remote_copy(
+            src_ref=src, dst_ref=dst, send_sem=ssem, recv_sem=rsem, device_id=where, device_id_type=MESH
+        )
+        held.append(copy)
+        return copy
+
+    spans = []
+    for l in range(layers):
+        at = l * per
+        for size in (3 * ch, ch + 2 * SPAN, 2 * SPAN, 2 * SPAN, ff):
+            spans.append(pl.ds(at, size))
+            at += size
+
+    class Weights:
+        def __init__(self, k):
+            self.k, self.where, self.stage = k, spans[k], 0
+
+        def block(self, uu, vv, r=slice(None)):
+            px, py = place(uu, vv)
+            return w_ref.at[px, py, c, r, self.where]
+
+        def move(self, ref, n, where):
+            return send(ref, ref, w_send.at[self.k, n], w_recv.at[self.k, n], where)
+
+        def move_row(self, vv, lo, hi, n, where):
+            def make(core):
+                ref = chunk_of(w_ref, core, vv, lo, hi, self.where)
+                return ref, ref
+
+            return send_either(make, w_send.at[self.k, n], w_recv.at[self.k, n], where)
+
+        def step(self):
+            stage, self.stage = self.stage, self.stage + 1
+            if stage == 0:
+                self.a0 = self.move(self.block(u, v), 0, u_next)
+                self.a1 = self.move(self.block(u, v), 1, u_prev)
+            elif stage == 1:
+                self.a0.wait_recv()
+                self.a2 = self.move(self.block(up, v, pl.ds(0, 16)), 2, u_next)
+                self.a1.wait_recv()
+                self.a3 = self.move(self.block(un, v, pl.ds(16, 16)), 3, u_prev)
+            elif stage == 2:
+                self.a2.wait_recv()
+                self.a3.wait_recv()
+                self.b0 = self.move_row(v, 0, 4, 4, v_next)
+                self.b1 = self.move_row(v, 0, 4, 5, v_prev)
+                self.p0 = self.move_row(v, 0, 4, 8, pair)
+            elif stage == 3:
+                self.b0.wait_recv()
+                self.b2 = self.move_row(vp, 0, 2, 6, v_next)
+                self.b1.wait_recv()
+                self.b3 = self.move_row(vn, 2, 4, 7, v_prev)
+                self.p1 = self.move_row(vp, 0, 4, 9, pair)
+                self.p2 = self.move_row(vn, 0, 4, 10, pair)
+            elif stage == 4:
+                self.b2.wait_recv()
+                self.b3.wait_recv()
+                self.p3 = self.move_row(vo, 0, 4, 11, pair)
+            else:
+                for copy in (self.p0, self.p1, self.p2, self.p3):
+                    copy.wait_recv()
+
+    class Sums:
+        def __init__(self, l, k, where):
+            self.l, self.k, self.where, self.stage = l, k, where, 0
+            self.total = pl.ds(l * per + where.start, where.size)
+            self.first = l == layers - 1
+            self.sent = []
+
+        def send(self, src, dst, n, where):
+            copy = pltpu.make_async_remote_copy(
+                src_ref=src,
+                dst_ref=dst,
+                send_sem=g_send.at[self.l, self.k, n],
+                recv_sem=g_recv.at[self.l, self.k, n],
+                device_id=where,
+                device_id_type=MESH,
+            )
+            copy.start()
+            self.sent.append(copy)
+            return copy
+
+        def far(self, vv, lo, n, where):
+            def make(core):
+                return chunk_of(gw_ref, core, vv, lo, lo + 2, self.where), from_far.at[n - 1, :, :, self.where]
+
+            copy = send_either(make, g_send.at[self.l, self.k, n], g_recv.at[self.l, self.k, n], where, self.sent)
+            return copy
+
+        def near(self, uu, r, n, where):
+            px, py = place(uu, v)
+            return self.send(gw_ref.at[px, py, c, r, self.where], from_near.at[n - 7, :, self.where], n, where)
+
+        def add_far(self, vv, lo, slots):
+            for i in range(2):
+                px, py = place(lo + i, vv)
+                value = gw_ref[px, py, c, :, self.where].astype(F32)
+                for slot in slots:
+                    value += from_far[slot, i, :, self.where].astype(F32)
+                gw_ref[px, py, c, :, self.where] = value.astype(BF)
+
+        def add_near(self, uu, r, slots):
+            px, py = place(uu, v)
+            value = gw_ref[px, py, c, r, self.where].astype(F32)
+            for slot in slots:
+                value += from_near[slot, :, self.where].astype(F32)
+            return value
+
+        def allow(self, kind, devices):
+            if self.first:
+                for where in devices:
+                    pl.semaphore_signal(credit.at[self.k, kind], inc=1, device_id=where, device_id_type=MESH)
+
+        def ask(self, kind, count):
+            if not self.first:
+                pl.semaphore_wait(credit.at[self.k, kind], count)
+
+        def step(self):
+            stage, self.stage = self.stage, self.stage + 1
+            upper, lower = pl.ds(0, 16), pl.ds(16, 16)
+            if stage == 0:
+                self.ask(0, 1)
+                self.q = self.send(
+                    gw_ref.at[:, :, 1 - c, :, self.where], from_pair.at[:, :, :, self.where], 0, pair
+                )
+            elif stage == 1:
+                self.q.wait_recv()
+
+                @pl.loop(0, 4)
+                def _(i):
+                    gw_ref[i, :, c, :, self.where] = (
+                        gw_ref[i, :, c, :, self.where].astype(F32) + from_pair[i, :, :, self.where].astype(F32)
+                    ).astype(BF)
+
+                self.allow(0, [pair])
+                self.ask(1, 2)
+                self.f0 = self.far(vo, 0, 1, v_next)
+                self.f1 = self.far(vo, 2, 2, v_prev)
+                self.f2 = self.far(vn, 2, 3, v_next)
+                self.f3 = self.far(vp, 0, 4, v_prev)
+            elif stage == 2:
+                self.f0.wait_recv()
+                self.add_far(vn, 0, [0])
+                self.f4 = self.far(vn, 0, 5, v_next)
+                self.f1.wait_recv()
+                self.add_far(vp, 2, [1])
+                self.f5 = self.far(vp, 2, 6, v_prev)
+            elif stage == 3:
+                for copy in (self.f2, self.f3, self.f4, self.f5):
+                    copy.wait_recv()
+                self.add_far(v, 0, [3, 4])
+                self.add_far(v, 2, [2, 5])
+                self.allow(1, [v_next, v_prev])
+                self.ask(2, 2)
+                self.n0 = self.near(uo, upper, 7, u_next)
+                self.n1 = self.near(uo, lower, 8, u_prev)
+                self.n2 = self.near(un, lower, 9, u_next)
+                self.n3 = self.near(up, upper, 10, u_prev)
+            elif stage == 4:
+                self.n0.wait_recv()
+                px, py = place(un, v)
+                gw_ref[px, py, c, upper, self.where] = self.add_near(un, upper, [0]).astype(BF)
+                self.n4 = self.near(un, upper, 11, u_next)
+                self.n1.wait_recv()
+                px, py = place(up, v)
+                gw_ref[px, py, c, lower, self.where] = self.add_near(up, lower, [1]).astype(BF)
+                self.n5 = self.near(up, lower, 12, u_prev)
+            else:
+                for copy in (self.n2, self.n3, self.n4, self.n5):
+                    copy.wait_recv()
+                final_ref[0:16, self.total] = self.add_near(u, upper, [3, 4])
+                final_ref[16:32, self.total] = self.add_near(u, lower, [2, 5])
+                self.allow(2, [u_next, u_prev])
+                for copy in self.sent:
+                    copy.wait_send()
+
+    fetches = [Weights(k) for k in range(len(spans))]
+    fetched = [0]
+    sums = []
+
+    def tick():
+        t = fetched[0]
+        if t < len(fetches) + 5:
+            fetched[0] += 1
+            for k, fetch in enumerate(fetches):
+                if 0 <= t - k < 6:
+                    fetch.step()
+        for total in sums:
+            if total.stage < 6:
+                total.step()
+
+    def need(l, part_index):
+        while fetches[5 * l + part_index].stage < 6:
+            tick()
+
+    def ready(l, k, at, size):
+        total = Sums(l, k, pl.ds(at, size))
+        total.step()
+        sums.append(total)
+
+    def clear(k):
+        for total in sums:
+            if total.k == k:
+                while total.stage < 6:
+                    tick()
+
+    def weight(where):
+        return w_ref[:, :, :, :, where].reshape(width, where.size)
+
+    def weight_rows(who, where):
+        return w_ref[who, :, :, :, where].reshape(ch, where.size)
+
+    w_ref[x, y, c] = mine_ref[...]
+    tick()
 
     class Gather:
         def __init__(self, i, block):
@@ -172,17 +432,15 @@
         return as_column(total[0:1])
 
     def columns(at, j, size=SPAN):
-        return pl.ds(pl.multiple_of(at + j * size, 128), size)
-
-    def weight_grad(left_index, spans):
+        return pl.ds(at + j * size, size)
+
+    def turn(left_index):
         turned[...] = rows[left_index].T
-        for right_ref, lead, width_r, at in spans:
-            size = SPAN if width_r % SPAN == 0 else width_r
-
-            @pl.loop(0, width_r // size)
-            def _(j, right_ref=right_ref, lead=lead, at=at, size=size):
-                right = right_ref[lead, :, columns(0, j, size)]
-                gw_ref[:, columns(at, j, size)] = nn(turned[...], right).astype(BF)
+
+    def weight_grad(l, k, right_ref, lead, start, size, at):
+        clear(k)
+        piece = nn(turned[...], right_ref[lead, :, start : start + size]).astype(BF)
+        gw_ref[:, :, :, :, at : at + size] = piece.reshape(4, 4, 2, 32, size)
 
     def norm_forward(k, h, gain):
         total = row_total(k, h * h)
@@ -204,18 +462,21 @@
     cot_gather = None
     for l in range(layers):
         base = l * per
-        at_exit, at_gate, at_up, at_down = base + 3 * ch, base + 4 * ch, base + 4 * ch + ff, base + 4 * ch + 2 * ff
+        at_exit, at_gate, at_down = base + 3 * ch, base + 4 * ch, base + 4 * ch + 2 * ff
         n1 = norm_forward(2 * l, hidden, gain_ref[l, 0:1])
         gather = Gather(2 * l, n1)
         if l == 0:
             cot_gather = Gather(2 * layers + 2 * (layers - 1), cot_ref[...].astype(BF))
+        tick()
         gather.pass_on()
+        tick()
         gather.finish()
         if l == 0:
             cot_gather.pass_on()
+        need(l, 0)
         full = rows[2 * l]
-        bm = nn(full, w_ref[:, columns(base, 0, ch)])
-        xm = nn(full, w_ref[:, columns(base, 2, ch)])
+        bm = nn(full, weight(columns(base, 0, ch)))
+        xm = nn(full, weight(columns(base, 2, ch)))
         bx = bm * xm
         ext[l, 8:] = bx
         tail = send(
@@ -223,8 +484,9 @@
         )
         bcx[l, 0] = bm
         bcx[l, 2] = xm
-        cm = nn(full, w_ref[:, columns(base, 1, ch)])
+        cm = nn(full, weight(columns(base, 1, ch)))
         bcx[l, 1] = cm
+        tick()
         tail.wait_recv()
         head = ext[l, 0:8]
         ext[l, 0:8] = jnp.where(s > 0, head, jnp.zeros_like(head))
@@ -234,69 +496,85 @@
         gated[l] = (cm * zc).astype(BF)
 
         def exit_piece(who, l=l, at=at_exit):
-            return nt(gated[l], w_ref[own_rows(who), columns(at, 0, ch)])
-
+            return nt(gated[l], weight_rows(who, columns(at, 0, ch)))
+
+        need(l, 1)
         scatter = Scatter(2 * l, exit_piece)
+        tick()
         scatter.pass_on()
+        tick()
         mid = hidden + scatter.finish()
         n2 = norm_forward(2 * l + 1, mid, gain_ref[l, 1:2])
         gather = Gather(2 * l + 1, n2)
+        tick()
         gather.pass_on()
+        tick()
         gather.finish()
-
-        @pl.loop(0, ff // SPAN)
-        def _(j, l=l, at_gate=at_gate, at_up=at_up):
-            full = rows[2 * l + 1]
-            g = nn(full, w_ref[:, columns(at_gate, j)])
-            u = nn(full, w_ref[:, columns(at_up, j)])
-            gates[l, :, columns(0, j)] = g
-            ups[l, :, columns(0, j)] = u
-            acted[l, :, columns(0, j)] = (g * jax.nn.sigmoid(g) * u).astype(BF)
+        need(l, 1)
+
+        for j in range(ff // SPAN):
+            need(l, 1 + j)
+            both = nn(rows[2 * l + 1], weight(columns(at_gate, j, 2 * SPAN)))
+            gates[l, :, j * 2 * SPAN : (j + 1) * 2 * SPAN] = both
+            g, up_value = both[:, :SPAN], both[:, SPAN:]
+            acted[l, :, j * SPAN : (j + 1) * SPAN] = (g * jax.nn.sigmoid(g) * up_value).astype(BF)
 
         def down_piece(who, l=l, at=at_down):
-            return nt(acted[l], w_ref[own_rows(who), columns(at, 0, ff)])
-
+            return nt(acted[l], weight_rows(who, columns(at, 0, ff)))
+
+        need(l, 4)
         scatter = Scatter(2 * l + 1, down_piece)
+        tick()
         scatter.pass_on()
+        tick()
         hidden = mid + scatter.finish()
     out_ref[...] = hidden
 
     grad = cot_ref[...]
     for l in reversed(range(layers)):
         base = l * per
-        at_exit, at_gate, at_up, at_down = base + 3 * ch, base + 4 * ch, base + 4 * ch + ff, base + 4 * ch + 2 * ff
+        at_exit, at_gate, at_down = base + 3 * ch, base + 4 * ch, base + 4 * ch + 2 * ff
         ie = 2 * layers + 2 * l
         if l == layers - 1:
             gather = cot_gather
         else:
             gather = Gather(ie, grad.astype(BF))
+            tick()
             gather.pass_on()
+            tick()
         gather.finish()
 
-        @pl.loop(0, ff // SPAN)
-        def _(j, l=l, ie=ie, at_down=at_down):
-            ds = nn(rows[ie], w_ref[:, columns(at_down, j)])
-            g = gates[l, :, columns(0, j)]
-            u = ups[l, :, columns(0, j)]
+        for j in range(ff // SPAN):
+            ds = nn(rows[ie], weight(columns(at_down, j)))
+            g = gates[l, :, j * 2 * SPAN : j * 2 * SPAN + SPAN]
+            up_value = gates[l, :, j * 2 * SPAN + SPAN : (j + 1) * 2 * SPAN]
             sig = jax.nn.sigmoid(g)
-            dgs[0, :, columns(0, j)] = (ds * u * sig * (1.0 + g * (1.0 - sig))).astype(BF)
-            dus[0, :, columns(0, j)] = (ds * (g * sig)).astype(BF)
-
-        def norm2_piece(who, at_gate=at_gate, at_up=at_up):
-            return nt(dgs[0], w_ref[own_rows(who), columns(at_gate, 0, ff)]) + nt(
-                dus[0], w_ref[own_rows(who), columns(at_up, 0, ff)]
-            )
+            dgates[0, :, j * 2 * SPAN : j * 2 * SPAN + SPAN] = (
+                ds * up_value * sig * (1.0 + g * (1.0 - sig))
+            ).astype(BF)
+            dgates[0, :, j * 2 * SPAN + SPAN : (j + 1) * 2 * SPAN] = (ds * (g * sig)).astype(BF)
+
+        def norm2_piece(who, at_gate=at_gate):
+            return nt(dgates[0], weight_rows(who, columns(at_gate, 0, 2 * ff)))
 
         scatter = Scatter(2 * layers + 2 * l, norm2_piece)
-        weight_grad(ie, [(acted, l, ff, at_down)])
+        turn(ie)
+        weight_grad(l, 4, acted, l, 0, ff, 4 * ch + 2 * ff)
         scatter.pass_on()
-        weight_grad(2 * l + 1, [(dgs, 0, ff, at_gate), (dus, 0, ff, at_up)])
+        ready(l, 4, 4 * ch + 2 * ff, ff)
+        turn(2 * l + 1)
+        for j in range(ff // SPAN):
+            weight_grad(l, 1 + j, dgates, 0, j * 2 * SPAN, 2 * SPAN, 4 * ch + j * 2 * SPAN)
+            tick()
+            ready(l, 1 + j, 4 * ch + j * 2 * SPAN, 2 * SPAN)
         dn2 = scatter.finish()
         dmid = grad + norm_backward(2 * l + 1, dn2, gain_ref[l, 1:2], 3 * layers + 2 * l + 1)
         gather = Gather(ie + 1, dmid.astype(BF))
+        tick()
         gather.pass_on()
+        tick()
         gather.finish()
-        dy = nn(rows[ie + 1], w_ref[:, columns(at_exit, 0, ch)])
+        dy = nn(rows[ie + 1], weight(columns(at_exit, 0, ch)))
         dz = dy * bcx[l, 1]
         dext[l, :tokens] = dz
         tail = send(
@@ -309,7 +587,8 @@
         dproj[0, :, ch : 2 * ch] = (dy * conv[l]).astype(BF)
         for j in range(3):
             small_ref[pl.ds(3 * l + j, 1), :] = jnp.sum(dz * ext[l, 6 + j : 6 + j + tokens], axis=0, keepdims=True)
-        weight_grad(ie + 1, [(gated, l, ch, at_exit)])
+        turn(ie + 1)
+        weight_grad(l, 0, gated, l, 0, ch, 3 * ch)
         tail.wait_recv()
         last = dext[l, tokens:]
         dext[l, tokens:] = jnp.where(s < seqs - 1, last, jnp.zeros_like(last))
@@ -319,23 +598,45 @@
         dproj[0, :, 2 * ch :] = (dbx * bcx[l, 0]).astype(BF)
 
         def norm1_piece(who, base=base):
-            return nt(dproj[0], w_ref[own_rows(who), columns(base, 0, 3 * ch)])
+            return nt(dproj[0], weight_rows(who, columns(base, 0, 3 * ch)))
 
         scatter = Scatter(2 * layers + 2 * l + 1, norm1_piece)
+        turn(2 * l)
+        weight_grad(l, 0, dproj, 0, 0, 3 * ch, 0)
         scatter.pass_on()
-        weight_grad(2 * l, [(dproj, 0, 3 * ch, base)])
+        ready(l, 0, 0, 4 * ch)
         dn1 = scatter.finish()
         grad = dmid + norm_backward(2 * l, dn1, gain_ref[l, 0:1], 3 * layers + 2 * l)
     din_ref[...] = grad
+    own = tally.at[0, 0]
+    tally[0, 0] = small_ref[...]
+    copy = send(own, tally.at[0, 1], t_send.at[0], t_recv.at[0], pair)
+    tick()
+    copy.wait_recv()
+    tally[1, x] = tally[0, 0] + tally[0, 1]
+    stages = ((1, x, lambda k: (lax.rem(x + k, 4) * 8 + y * 2 + c, z)), (2, y, lambda k: (x * 8 + lax.rem(y + k, 4) * 2 + c, z)))
+    for n, here, where in stages:
+        slot = tally.at[n, here]
+        copies = [send(slot, slot, t_send.at[3 * n - 3 + k], t_recv.at[3 * n - 3 + k], where(k)) for k in (1, 2, 3)]
+        tick()
+        for copy in copies:
+            copy.wait_recv()
+        total = tally[n, 0] + tally[n, 1] + tally[n, 2] + tally[n, 3]
+        if n == 1:
+            tally[2, y] = total
+        else:
+            small_ref[...] = total
+    while any(total.stage < 6 for total in sums):
+        tick()
     for copy in pending:
         copy.wait_send()
 
 
-def run_step(x, cot, w, kern, gain, seqs):
+def run_step(x, cot, mine, kern, gain, seqs):
     layers, taps, ch = kern.shape
     tokens = x.shape[0]
-    width = w.shape[0]
-    per = w.shape[1] // layers
+    width = 4 * ch
+    per = mine.shape[1] // layers
     ff = (per - 4 * ch) // 3
     n = 4 * layers
     vmem = pl.BlockSpec(memory_space=pltpu.VMEM)
@@ -345,7 +646,7 @@
         out_shape=(
             jax.ShapeDtypeStruct((tokens, ch), F32),
             jax.ShapeDtypeStruct((tokens, ch), F32),
-            jax.ShapeDtypeStruct(w.shape, BF),
+            jax.ShapeDtypeStruct(mine.shape, F32),
             jax.ShapeDtypeStruct((16, ch), F32),
         ),
         in_specs=[vmem] * 5,
@@ -363,13 +664,17 @@
             pltpu.VMEM((layers, 3, tokens, ch), F32),
             pltpu.VMEM((layers, tokens, ch), F32),
             pltpu.VMEM((layers, tokens, ch), BF),
-            pltpu.VMEM((layers, tokens, ff), F32),
-            pltpu.VMEM((layers, tokens, ff), F32),
+            pltpu.VMEM((layers, tokens, 2 * ff), F32),
             pltpu.VMEM((layers, tokens, ff), BF),
-            pltpu.VMEM((1, tokens, ff), BF),
-            pltpu.VMEM((1, tokens, ff), BF),
+            pltpu.VMEM((1, tokens, 2 * ff), BF),
             pltpu.VMEM((1, tokens, 3 * ch), BF),
             pltpu.VMEM((width, tokens), BF),
+            pltpu.VMEM((4, 4, 2, 32, layers * per), BF),
+            pltpu.VMEM((4, 4, 2, 32, per), BF),
+            pltpu.VMEM((4, 4, 32, per), BF),
+            pltpu.VMEM((6, 2, 32, per), BF),
+            pltpu.VMEM((6, 16, per), BF),
+            pltpu.VMEM((3, 4, 16, ch), F32),
             dma((n, 6)),
             dma((n, 6)),
             dma((n, 6)),
@@ -378,12 +683,19 @@
             dma((n, 3)),
             dma((2 * layers,)),
             dma((2 * layers,)),
+            dma((5 * layers, 12)),
+            dma((5 * layers, 12)),
+            dma((layers, 5, 13)),
+            dma((layers, 5, 13)),
+            dma((7,)),
+            dma((7,)),
+            pltpu.SemaphoreType.REGULAR((5, 3)),
         ],
         compiler_params=pltpu.CompilerParams(
-            collective_id=0, has_side_effects=True, vmem_limit_bytes=62 * 1024 * 1024
+            collective_id=0, has_side_effects=True, vmem_limit_bytes=67043328
         ),
         name="layers",
-    )(x, cot, w, kern, gain)
+    )(x, cot, mine, kern, gain)
 
 
 def adamw(weight, grad, first, second, rate, decay):
@@ -394,10 +706,13 @@
 
 
 def laid_out(entry, leave, gates, down):
-    layers = entry.shape[0]
+    layers, ff = entry.shape[0], gates.shape[3]
     parts = []
     for l in range(layers):
-        parts += [entry[l, 0], entry[l, 1], entry[l, 2], leave[l].T, gates[l, 0], gates[l, 1], down[l].T]
+        parts += [entry[l, 0], entry[l, 1], entry[l, 2], leave[l].T]
+        for j in range(0, ff, SPAN):
+            parts += [gates[l, 0, :, j : j + SPAN], gates[l, 1, :, j : j + SPAN]]
+        parts.append(down[l].T)
     return jnp.concatenate(parts, axis=1)
 
 
@@ -409,7 +724,11 @@
         entry.append(jnp.stack([flat[:, b + c * ch : b + (c + 1) * ch] for c in range(3)]))
         leave.append(flat[:, b + 3 * ch : b + 4 * ch].T)
         g = b + 4 * ch
-        gates.append(jnp.stack([flat[:, g : g + ff], flat[:, g + ff : g + 2 * ff]]))
+        halves = [
+            jnp.concatenate([flat[:, g + 2 * j + k : g + 2 * j + k + SPAN] for j in range(0, ff, SPAN)], axis=1)
+            for k in (0, SPAN)
+        ]
+        gates.append(jnp.stack(halves))
         down.append(flat[:, g + 2 * ff : g + 3 * ff].T)
     return tuple(jnp.stack(v) for v in (entry, leave, gates, down))
 
@@ -442,10 +761,7 @@
     mine = laid_out(
         entry_weight.astype(BF), exit_weight.astype(BF), gate_up.astype(BF), down_weight.astype(BF)
     )
-    whole = lax.all_gather(mine, "seq", axis=0, tiled=True)
-    hidden, grad, terms, small = run_step(inputs, cotangent, whole, conv_kernel, norm_gain, seqs)
-    summed = lax.psum_scatter(terms, "seq", scatter_dimension=0, tiled=True).astype(F32)
-    small = lax.psum(small, "seq")
+    hidden, grad, summed, small = run_step(inputs, cotangent, mine, conv_kernel, norm_gain, seqs)
     entry_grad, exit_grad, gate_grad, down_grad = taken_apart(summed, layers, ch, ff)
     kernel_grad = small[: 3 * layers].reshape(layers, 3, ch)
     gain_grad = small[3 * layers : 5 * layers].reshape(layers, 2, ch)

time: 426 us -> 275 us (0.65)
  blocking collectives: 128 us -> 0 us
  waiting for transfers between devices: 78 us -> 0 us
  Pallas kernels: 188 us -> 243 us
  between operations: 14.4 us -> 0.96 us
  local copies, waits for them, and re-layouts: 7.9 us -> 20.3 us
    psum x1 -> x0, blocking collectives: 128 us -> none  [per_device(): small = lax.psum(small, 'seq')]
    all_gather x1 -> x0, waiting for transfers between devices: 78 us -> none  [per_device(): whole = lax.all_gather(mine, 'seq', axis=0, tiled=True)]
    pallas_call x1, Pallas kernels: 188 us -> 243 us  [run_step(): pl.pallas_call(functools.partial(step_kernel, (layers, seqs, tokens, ch,...]
    unnamed x66 -> x72, local copies, waits for them, and re-layouts: 7.77 us -> 18.6 us
  transfers between devices with their start and end apart: 2 -> 0, of which waited for: 1 -> 0; matrix products, arithmetic and copies ran while one was open for 1% -> 0% of each run, Pallas kernels for 0% -> 0%
where the time goes in v2:
time: 275 us; the launch traced here: 274 us
  Pallas kernels  243 us (88%)
  local copies, waits for them, and re-layouts  20.3 us (7%)
  other arithmetic  9.15 us (3%)
    pallas_call x1, Pallas kernels, run_step(): pl.pallas_call(functools.partial(step_kernel, (layers, seqs, tokens, ch,...  243 us
    unnamed x72, local copies, waits for them, and re-layouts  18.6 us
    sub x6, other arithmetic, adamw(): return (weight - rate * (update + decay * weight), first_new, second_new)  6.09 us

profile of v2, /device:TPU:0, one launch (start us, length us, event | category | flops | bytes accessed | tf_op | source)
XLA Modules:
  0.0 273.9 jit_solution(6660666010486735924)
XLA Ops:
  0.7 1.0 convert_element_type.12
  1.7 0.6 constant_dynamic-update-slice_fusion.19
  2.9 0.6 constant_dynamic-update-slice_fusion.17
  3.5 0.8 convert_element_type.13
  4.3 0.6 constant_dynamic-update-slice_fusion.16
  4.9 1.1 convert_element_type.14
  6.1 0.6 constant_dynamic-update-slice_fusion.15
  6.7 0.6 constant_dynamic-update-slice_fusion.14
  7.3 0.6 constant_dynamic-update-slice_fusion.13
  7.9 0.6 constant_dynamic-update-slice_fusion.12
  8.5 0.6 constant_dynamic-update-slice_fusion.11
  9.1 0.6 constant_dynamic-update-slice_fusion.10
  9.7 0.6 fusion.4
  10.4 0.6 constant_dynamic-update-slice_fusion.9
  11.0 0.6 constant_dynamic-update-slice_fusion.8
  12.8 0.6 constant_dynamic-update-slice_fusion.5
  13.4 0.6 constant_dynamic-update-slice_fusion.4
  14.0 0.6 constant_dynamic-update-slice_fusion.3
  14.7 0.6 constant_dynamic-update-slice_fusion.2
  15.3 0.6 constant_dynamic-update-slice_fusion.1
  15.9 0.6 constant_dynamic-update-slice_fusion
  16.5 0.6 fusion.3.mine_ref
  17.7 243.5 %layers.1 = (f32[256,256]{1,0:T(8,128)}, f32[256,256]{1,0:T(8,128)}, f32[32,8960]{1,0:T(8,128)}, f32[16,256]{1,0:T(8,128)}) custom-call(f32[256,256]{1,0:T(8,128)} %x_ref.1, f32[256,256]{1,0:T(8,128)} %cot_ref.1, bf16[32,8960]{1,0:T(8,128)(2,1)} %fusion.3.mine_ref, f32[2,3,256]{2,1,0:T(4,128)} %copy.51.kern_ref, f32[2,2,256]{2,1,0:T(2,128)} %gain_ref.1), custom_call_target="tpu_custom_call" | custom-call | tf_op jit(solution)/shard_map/layers/pallas_call | solution.py:644
  261.2 0.9 slice_bitcast_fusion.5
  262.2 2.1 multiply_subtract_fusion.2
  264.4 0.7 multiply_subtract_fusion.3
  265.3 0.9 copy-done
  266.6 1.5 multiply_subtract_fusion
  268.3 1.1 multiply_subtract_fusion.1
  270.6 0.6 multiply_subtract_fusion.5
  272.5 0.7 copy.92
  273.2 0.7 copy.93
  (64 shorter events, 5.5 us)
Async XLA Ops:
  0.7 9.1 %copy-start.1 = (f32[2,1152,32]{1,2,0:T(8,128)S(1)}, f32[2,1152,32]{1,2,0:T(8,128)}, u32[]{:S(2)}) copy-start(f32[2,1152,32]{1,2,0:T(8,128)} %param.25) | copy-start | bytes 884740
  4.9 12.2 %copy-start.13 = (f32[2,3,256]{2,0,1:T(2,128)S(1)}, f32[2,3,256]{2,0,1:T(2,128)}, u32[]{:S(2)}) copy-start(f32[2,3,256]{2,0,1:T(2,128)} %param.26) | copy-start | bytes 18436
  261.2 3.2 %copy-start.10 = (f32[2,256,32]{1,2,0:T(8,128)S(1)}, f32[2,256,32]{1,2,0:T(8,128)}, u32[]{:S(2)}) copy-start(f32[2,256,32]{1,2,0:T(8,128)} %param.23) | copy-start | bytes 196612
  261.2 3.1 %copy-start.11 = (f32[2,256,32]{1,2,0:T(8,128)S(1)}, f32[2,256,32]{1,2,0:T(8,128)}, u32[]{:S(2)}) copy-start(f32[2,256,32]{1,2,0:T(8,128)} %param.30) | copy-start | bytes 196612
  261.2 3.1 %copy-start.12 = (f32[2,256,32]{1,2,0:T(8,128)S(1)}, f32[2,256,32]{1,2,0:T(8,128)}, u32[]{:S(2)}) copy-start(f32[2,256,32]{1,2,0:T(8,128)} %param.31) | copy-start | bytes 196612
  262.2 2.9 %copy-start.3 = (f32[32,8960]{1,0:T(8,128)S(1)}, f32[32,8960]{1,0:T(8,128)}, u32[]{:S(2)}) copy-start(f32[32,8960]{1,0:T(8,128)} %get-tuple-element.32) | copy-start | bytes 3440644
  265.1 1.1 copy-start
  265.2 1.2 copy-start.4
  265.2 1.4 copy-start.5
  266.6 1.6 copy-start.2
  266.6 1.6 copy-start.6
  266.6 1.6 copy-start.7
  268.2 1.2 copy-start.17
  268.2 1.8 copy-start.14
  268.2 1.8 copy-start.18
  268.2 1.8 copy-start.19
  268.2 2.4 copy-start.15
  268.2 2.4 copy-start.20
  268.2 2.4 copy-start.21
  268.2 4.2 %copy-start.9 = (f32[256,256]{1,0:T(8,128)S(1)}, f32[256,256]{1,0:T(8,128)}, u32[]{:S(2)}) copy-start(f32[256,256]{1,0:T(8,128)} %get-tuple-element.162) | copy-start | bytes 786436
  268.3 4.9 %copy-start.8 = (f32[256,256]{1,0:T(8,128)S(1)}, f32[256,256]{1,0:T(8,128)}, u32[]{:S(2)}) copy-start(f32[256,256]{1,0:T(8,128)} %get-tuple-element.163) | copy-start | bytes 786436
  270.0 3.9 %copy-start.16 = (f32[2,2,256]{2,1,0:T(2,128)}, f32[2,2,256]{2,1,0:T(2,128)S(1)}, u32[]{:S(2)}) copy-start(f32[2,2,256]{2,1,0:T(2,128)S(1)} %reshape.59) | copy-start | bytes 12292

commit v3 on v2

--- a/solution.py
+++ b/solution.py
@@ -31,7 +31,10 @@
     cfg,
     x_ref,
     cot_ref,
-    mine_ref,
+    entry_ref,
+    exit_ref,
+    gate_ref,
+    down_ref,
     kern_ref,
     gain_ref,
     out_ref,
@@ -156,6 +159,28 @@
             spans.append(pl.ds(at, size))
             at += size
 
+    def pack(k):
+        l, part_index = k // 5, k % 5
+        at = l * per
+
+        def put(start, value):
+            w_ref[x, y, c, :, start : start + value.shape[1]] = value.astype(BF)
+
+        if part_index == 0:
+            for j in range(3):
+                put(at + j * ch, entry_ref[l, j])
+        elif part_index == 4:
+            put(at + 4 * ch + 2 * ff, down_ref[l])
+        else:
+            if part_index == 1:
+                put(at + 3 * ch, exit_ref[l])
+            j = part_index - 1
+            for half_index in range(2):
+                put(
+                    at + 4 * ch + (2 * j + half_index) * SPAN,
+                    gate_ref[l, half_index, :, j * SPAN : (j + 1) * SPAN],
+                )
+
     class Weights:
         def __init__(self, k):
             self.k, self.where, self.stage = k, spans[k], 0
@@ -177,6 +202,7 @@
         def step(self):
             stage, self.stage = self.stage, self.stage + 1
             if stage == 0:
+                pack(self.k)
                 self.a0 = self.move(self.block(u, v), 0, u_next)
                 self.a1 = self.move(self.block(u, v), 1, u_prev)
             elif stage == 1:
@@ -355,7 +381,6 @@
     def weight_rows(who, where):
         return w_ref[who, :, :, :, where].reshape(ch, where.size)
 
-    w_ref[x, y, c] = mine_ref[...]
     tick()
 
     class Gather:
@@ -418,44 +443,50 @@
             lower = part[3] + landed[i, 2].astype(F32) + landed[i, 5].astype(F32)
             return jnp.concatenate([upper, lower], axis=0)
 
-    def row_total(i, value):
-        sums = jnp.sum(value, axis=1, keepdims=True)
-        stats[i, z] = jnp.broadcast_to(sums, (tokens, 128)).T[0:8]
-        there = stats.at[i, z]
-        got = [
-            send(there, there, st_send.at[i, k], st_recv.at[i, k], (s, who))
-            for k, who in enumerate((zr, zl, zo))
-        ]
-        for c in got:
-            c.wait_recv()
-        total = stats[i, 0] + stats[i, 1] + stats[i, 2] + stats[i, 3]
-        return as_column(total[0:1])
+    class Total:
+        def __init__(self, i, sums):
+            self.i = i
+            stats[i, z] = jnp.broadcast_to(sums, (tokens, 128)).T[0:8]
+            there = stats.at[i, z]
+            self.got = [
+                send(there, there, st_send.at[i, k], st_recv.at[i, k], (s, who))
+                for k, who in enumerate((zr, zl, zo))
+            ]
+
+        def finish(self):
+            for copy in self.got:
+                copy.wait_recv()
+            i = self.i
+            total = stats[i, 0] + stats[i, 1] + stats[i, 2] + stats[i, 3]
+            return as_column(total[0:1])
+
+    def row_sum(value):
+        return jnp.sum(value, axis=1, keepdims=True)
 
     def columns(at, j, size=SPAN):
         return pl.ds(at + j * size, size)
 
-    def turn(left_index):
-        turned[...] = rows[left_index].T
+    def turn(left_index, k=None):
+        if k is None:
+            turned[...] = rows[left_index].T
+        else:
+            turned[...] = (rows[left_index].astype(F32) * scales[k][:, 0:1]).astype(BF).T
 
     def weight_grad(l, k, right_ref, lead, start, size, at):
         clear(k)
         piece = nn(turned[...], right_ref[lead, :, start : start + size]).astype(BF)
         gw_ref[:, :, :, :, at : at + size] = piece.reshape(4, 4, 2, 32, size)
 
-    def norm_forward(k, h, gain):
-        total = row_total(k, h * h)
-        scale = lax.rsqrt(total / width + EPS)
+    def norm_scale(k, total, h):
+        scale = lax.rsqrt(total.finish() / width + EPS)
         scales[k] = jnp.broadcast_to(scale, (tokens, 128))
-        a = h * scale
-        normed[k] = a
-        return (a * gain).astype(BF)
-
-    def norm_backward(k, dn, gain, small_row):
+        normed[k] = h * scale
+        return scale
+
+    def norm_backward(k, dn, inner, gain, small_row):
         a = normed[k]
-        t = dn * gain
         small_ref[pl.ds(small_row, 1), :] = jnp.sum(dn * a, axis=0, keepdims=True)
-        inner = row_total(2 * layers + k, t * a)
-        return scales[k][:, 0:1] * (t - a * (inner / width))
+        return scales[k][:, 0:1] * (dn * gain - a * (inner / width))
 
     small_ref[...] = jnp.zeros_like(small_ref)
     hidden = x_ref[...]
@@ -463,8 +494,8 @@
     for l in range(layers):
         base = l * per
         at_exit, at_gate, at_down = base + 3 * ch, base + 4 * ch, base + 4 * ch + 2 * ff
-        n1 = norm_forward(2 * l, hidden, gain_ref[l, 0:1])
-        gather = Gather(2 * l, n1)
+        gather = Gather(2 * l, (hidden * gain_ref[l, 0:1]).astype(BF))
+        total = Total(2 * l, row_sum(hidden * hidden))
         if l == 0:
             cot_gather = Gather(2 * layers + 2 * (layers - 1), cot_ref[...].astype(BF))
         tick()
@@ -473,10 +504,11 @@
         gather.finish()
         if l == 0:
             cot_gather.pass_on()
+        scale = norm_scale(2 * l, total, hidden)
         need(l, 0)
         full = rows[2 * l]
-        bm = nn(full, weight(columns(base, 0, ch)))
-        xm = nn(full, weight(columns(base, 2, ch)))
+        bm = nn(full, weight(columns(base, 0, ch))) * scale
+        xm = nn(full, weight(columns(base, 2, ch))) * scale
         bx = bm * xm
         ext[l, 8:] = bx
         tail = send(
@@ -484,7 +516,7 @@
         )
         bcx[l, 0] = bm
         bcx[l, 2] = xm
-        cm = nn(full, weight(columns(base, 1, ch)))
+        cm = nn(full, weight(columns(base, 1, ch))) * scale
         bcx[l, 1] = cm
         tick()
         tail.wait_recv()
@@ -504,17 +536,18 @@
         scatter.pass_on()
         tick()
         mid = hidden + scatter.finish()
-        n2 = norm_forward(2 * l + 1, mid, gain_ref[l, 1:2])
-        gather = Gather(2 * l + 1, n2)
+        gather = Gather(2 * l + 1, (mid * gain_ref[l, 1:2]).astype(BF))
+        total = Total(2 * l + 1, row_sum(mid * mid))
         tick()
         gather.pass_on()
         tick()
         gather.finish()
+        scale = norm_scale(2 * l + 1, total, mid)
         need(l, 1)
 
         for j in range(ff // SPAN):
             need(l, 1 + j)
-            both = nn(rows[2 * l + 1], weight(columns(at_gate, j, 2 * SPAN)))
+            both = nn(rows[2 * l + 1], weight(columns(at_gate, j, 2 * SPAN))) * scale
             gates[l, :, j * 2 * SPAN : (j + 1) * 2 * SPAN] = both
             g, up_value = both[:, :SPAN], both[:, SPAN:]
             acted[l, :, j * SPAN : (j + 1) * SPAN] = (g * jax.nn.sigmoid(g) * up_value).astype(BF)
@@ -544,15 +577,18 @@
             tick()
         gather.finish()
 
+        inner = jnp.zeros((tokens, 1), F32)
         for j in range(ff // SPAN):
             ds = nn(rows[ie], weight(columns(at_down, j)))
             g = gates[l, :, j * 2 * SPAN : j * 2 * SPAN + SPAN]
             up_value = gates[l, :, j * 2 * SPAN + SPAN : (j + 1) * 2 * SPAN]
             sig = jax.nn.sigmoid(g)
-            dgates[0, :, j * 2 * SPAN : j * 2 * SPAN + SPAN] = (
-                ds * up_value * sig * (1.0 + g * (1.0 - sig))
-            ).astype(BF)
-            dgates[0, :, j * 2 * SPAN + SPAN : (j + 1) * 2 * SPAN] = (ds * (g * sig)).astype(BF)
+            dg = (ds * up_value * sig * (1.0 + g * (1.0 - sig))).astype(BF)
+            du = (ds * (g * sig)).astype(BF)
+            dgates[0, :, j * 2 * SPAN : j * 2 * SPAN + SPAN] = dg
+            dgates[0, :, j * 2 * SPAN + SPAN : (j + 1) * 2 * SPAN] = du
+            inner += row_sum(dg.astype(F32) * g + du.astype(F32) * up_value)
+        total = Total(2 * layers + 2 * l + 1, inner)
 
         def norm2_piece(who, at_gate=at_gate):
             return nt(dgates[0], weight_rows(who, columns(at_gate, 0, 2 * ff)))
@@ -562,13 +598,12 @@
         weight_grad(l, 4, acted, l, 0, ff, 4 * ch + 2 * ff)
         scatter.pass_on()
         ready(l, 4, 4 * ch + 2 * ff, ff)
-        turn(2 * l + 1)
+        turn(2 * l + 1, 2 * l + 1)
         for j in range(ff // SPAN):
             weight_grad(l, 1 + j, dgates, 0, j * 2 * SPAN, 2 * SPAN, 4 * ch + j * 2 * SPAN)
-            tick()
             ready(l, 1 + j, 4 * ch + j * 2 * SPAN, 2 * SPAN)
         dn2 = scatter.finish()
-        dmid = grad + norm_backward(2 * l + 1, dn2, gain_ref[l, 1:2], 3 * layers + 2 * l + 1)
+        dmid = grad + norm_backward(2 * l + 1, dn2, total.finish(), gain_ref[l, 1:2], 3 * layers + 2 * l + 1)
         gather = Gather(ie + 1, dmid.astype(BF))
         tick()
         gather.pass_on()
@@ -588,25 +623,33 @@
         for j in range(3):
             small_ref[pl.ds(3 * l + j, 1), :] = jnp.sum(dz * ext[l, 6 + j : 6 + j + tokens], axis=0, keepdims=True)
         turn(ie + 1)
-        weight_grad(l, 0, gated, l, 0, ch, 3 * ch)
+        weight_grad(l, 5, gated, l, 0, ch, 3 * ch)
+        ready(l, 5, 3 * ch, ch)
+        tick()
         tail.wait_recv()
         last = dext[l, tokens:]
         dext[l, tokens:] = jnp.where(s < seqs - 1, last, jnp.zeros_like(last))
         k = kern_ref[l]
         dbx = k[2:3] * dext[l, 0:tokens] + k[1:2] * dext[l, 1 : 1 + tokens] + k[0:1] * dext[l, 2 : 2 + tokens]
-        dproj[0, :, :ch] = (dbx * bcx[l, 2]).astype(BF)
-        dproj[0, :, 2 * ch :] = (dbx * bcx[l, 0]).astype(BF)
+        db = (dbx * bcx[l, 2]).astype(BF)
+        dx = (dbx * bcx[l, 0]).astype(BF)
+        dproj[0, :, :ch] = db
+        dproj[0, :, 2 * ch :] = dx
+        dc = dproj[0, :, ch : 2 * ch].astype(F32)
+        inner = row_sum(db.astype(F32) * bcx[l, 0] + dc * bcx[l, 1] + dx.astype(F32) * bcx[l, 2])
+        total = Total(2 * layers + 2 * l, inner)
 
         def norm1_piece(who, base=base):
             return nt(dproj[0], weight_rows(who, columns(base, 0, 3 * ch)))
 
         scatter = Scatter(2 * layers + 2 * l + 1, norm1_piece)
-        turn(2 * l)
+        turn(2 * l, 2 * l)
         weight_grad(l, 0, dproj, 0, 0, 3 * ch, 0)
         scatter.pass_on()
-        ready(l, 0, 0, 4 * ch)
+        ready(l, 0, 0, 3 * ch)
+        tick()
         dn1 = scatter.finish()
-        grad = dmid + norm_backward(2 * l, dn1, gain_ref[l, 0:1], 3 * layers + 2 * l)
+        grad = dmid + norm_backward(2 * l, dn1, total.finish(), gain_ref[l, 0:1], 3 * layers + 2 * l)
     din_ref[...] = grad
     own = tally.at[0, 0]
     tally[0, 0] = small_ref[...]
@@ -632,12 +675,12 @@
         copy.wait_send()
 
 
-def run_step(x, cot, mine, kern, gain, seqs):
+def run_step(x, cot, weights, kern, gain, seqs):
     layers, taps, ch = kern.shape
     tokens = x.shape[0]
     width = 4 * ch
-    per = mine.shape[1] // layers
-    ff = (per - 4 * ch) // 3
+    ff = weights[2].shape[3]
+    per = 4 * ch + 3 * ff
     n = 4 * layers
     vmem = pl.BlockSpec(memory_space=pltpu.VMEM)
     dma = pltpu.SemaphoreType.DMA
@@ -646,10 +689,10 @@
         out_shape=(
             jax.ShapeDtypeStruct((tokens, ch), F32),
             jax.ShapeDtypeStruct((tokens, ch), F32),
-            jax.ShapeDtypeStruct(mine.shape, F32),
+            jax.ShapeDtypeStruct((32, layers * per), F32),
             jax.ShapeDtypeStruct((16, ch), F32),
         ),
-        in_specs=[vmem] * 5,
+        in_specs=[vmem] * 8,
         out_specs=(vmem,) * 4,
         scratch_shapes=[
             pltpu.VMEM((n, tokens, width), BF),
@@ -685,17 +728,17 @@
             dma((2 * layers,)),
             dma((5 * layers, 12)),
             dma((5 * layers, 12)),
-            dma((layers, 5, 13)),
-            dma((layers, 5, 13)),
+            dma((layers, 6, 13)),
+            dma((layers, 6, 13)),
             dma((7,)),
             dma((7,)),
-            pltpu.SemaphoreType.REGULAR((5, 3)),
+            pltpu.SemaphoreType.REGULAR((6, 3)),
         ],
         compiler_params=pltpu.CompilerParams(
             collective_id=0, has_side_effects=True, vmem_limit_bytes=67043328
         ),
         name="layers",
-    )(x, cot, mine, kern, gain)
+    )(x, cot, *weights, kern, gain)
 
 
 def adamw(weight, grad, first, second, rate, decay):
@@ -703,17 +746,6 @@
     second_new = 0.999 * second + 0.001 * grad * grad
     update = first_new / (1.0 - 0.9**STEP) / (jnp.sqrt(second_new / (1.0 - 0.999**STEP)) + 1e-08)
     return (weight - rate * (update + decay * weight), first_new, second_new)
-
-
-def laid_out(entry, leave, gates, down):
-    layers, ff = entry.shape[0], gates.shape[3]
-    parts = []
-    for l in range(layers):
-        parts += [entry[l, 0], entry[l, 1], entry[l, 2], leave[l].T]
-        for j in range(0, ff, SPAN):
-            parts += [gates[l, 0, :, j : j + SPAN], gates[l, 1, :, j : j + SPAN]]
-        parts.append(down[l].T)
-    return jnp.concatenate(parts, axis=1)
 
 
 def taken_apart(flat, layers, ch, ff):
@@ -758,10 +790,8 @@
     layers, _, _, ch = entry_weight.shape
     ff = gate_up.shape[3]
     seqs = lax.axis_size("seq")
-    mine = laid_out(
-        entry_weight.astype(BF), exit_weight.astype(BF), gate_up.astype(BF), down_weight.astype(BF)
-    )
-    hidden, grad, summed, small = run_step(inputs, cotangent, mine, conv_kernel, norm_gain, seqs)
+    weights = (entry_weight, jnp.swapaxes(exit_weight, 1, 2), gate_up, jnp.swapaxes(down_weight, 1, 2))
+    hidden, grad, summed, small = run_step(inputs, cotangent, weights, conv_kernel, norm_gain, seqs)
     entry_grad, exit_grad, gate_grad, down_grad = taken_apart(summed, layers, ch, ff)
     kernel_grad = small[: 3 * layers].reshape(layers, 3, ch)
     gain_grad = small[3 * layers : 5 * layers].reshape(layers, 2, ch)

time: 275 us -> 244 us (0.89)
  Pallas kernels: 243 us -> 227 us
  local copies, waits for them, and re-layouts: 20.3 us -> 9.55 us
  other arithmetic: 9.15 us -> 4.99 us
    pallas_call x1, Pallas kernels: 243 us -> 227 us  [run_step(): pl.pallas_call(functools.partial(step_kernel, (layers, seqs, tokens, ch,...]
    unnamed x72 -> x51, local copies, waits for them, and re-layouts: 18.6 us -> 6.47 us
    convert_element_type x4 -> x0, other arithmetic: 2.96 us -> none  [the longest x1 1.11 us: per_device(): gate_up.astype(BF)]
where the time goes in v3:
time: 244 us; the launch traced here: 242 us
  Pallas kernels  227 us (93%)
  local copies, waits for them, and re-layouts  9.55 us (4%)
  other arithmetic  4.99 us (2%)
    pallas_call x1, Pallas kernels, run_step(): pl.pallas_call(functools.partial(step_kernel, (layers, seqs, tokens, ch,...  227 us
    unnamed x51, local copies, waits for them, and re-layouts  6.47 us
    sub x6, other arithmetic, adamw(): return (weight - rate * (update + decay * weight), first_new, second_new)  4.88 us

profile of v3, /device:TPU:0, one launch (start us, length us, event | category | flops | bytes accessed | tf_op | source)
XLA Modules:
  0.0 242.3 jit_solution(8320927824439550369)
XLA Ops:
  0.7 1.3 copy.51.kern_ref
  2.0 226.8 %layers.1 = (f32[256,256]{1,0:T(8,128)}, f32[256,256]{1,0:T(8,128)}, f32[32,8960]{1,0:T(8,128)}, f32[16,256]{1,0:T(8,128)}) custom-call(f32[256,256]{1,0:T(8,128)} %x_ref.1, f32[256,256]{1,0:T(8,128)} %cot_ref.1, f32[2,3,32,256]{3,2,1,0:T(8,128)} %entry_ref.1, f32[2,32,256]{2,1,0:T(8,128)} %bitcast.47, f32[2,2,32,1152]{3,2,1,0:T(8,128)} %gate_ref.1, ...), custom_call_target="tpu_custom_call" | custom-call | tf_op jit(solution)/shard_map/layers/pallas_call | solution.py:687
  228.7 1.1 fusion.14
  229.8 0.0 copy-start
  229.9 0.0 copy-start.3
  229.9 0.0 copy-start.4
  230.0 0.9 copy-done
  230.9 0.2 copy-done.3
  231.1 0.2 copy-done.4
  231.3 1.5 multiply_subtract_fusion
  232.8 0.9 slice_bitcast_fusion.3
  233.8 0.0 copy-start.1
  233.8 0.0 copy-start.5
  233.8 0.0 copy-start.6
  233.8 0.9 multiply_subtract_fusion.2
  234.8 0.7 multiply_subtract_fusion.3
  235.5 1.0 slice_bitcast_fusion.1
  236.5 0.0 copy-start.14
  236.5 0.0 copy-start.18
  236.6 0.0 copy-start.19
  236.6 0.0 copy-start.15
  236.6 0.0 copy-start.20
  236.6 0.0 copy-start.21
  236.6 1.1 multiply_subtract_fusion.1
  237.8 0.6 copy.57
  238.4 0.6 copy.58
  239.0 0.6 copy.59
  239.6 0.0 copy-start.16
  239.6 0.6 multiply_subtract_fusion.5
  240.2 0.6 copy.56
  240.8 0.7 copy.71
  241.5 0.7 copy.72
  (38 shorter events, 0.2 us)
Async XLA Ops:
  229.8 1.1 copy-start
  229.9 1.2 copy-start.3
  229.9 1.4 copy-start.4
  231.3 2.5 %copy-start.2 = (f32[2,3,32,256]{3,2,1,0:T(8,128)S(1)}, f32[2,3,32,256]{3,2,1,0:T(8,128)}, u32[]{:S(2)}) copy-start(f32[2,3,32,256]{3,2,1,0:T(8,128)} %entry_ref.1) | copy-start | bytes 589828
  231.3 2.5 %copy-start.10 = (f32[2,3,32,256]{3,2,1,0:T(8,128)S(1)}, f32[2,3,32,256]{3,2,1,0:T(8,128)}, u32[]{:S(2)}) copy-start(f32[2,3,32,256]{3,2,1,0:T(8,128)} %param.28) | copy-start | bytes 589828
  231.3 2.5 %copy-start.11 = (f32[2,3,32,256]{3,2,1,0:T(8,128)S(1)}, f32[2,3,32,256]{3,2,1,0:T(8,128)}, u32[]{:S(2)}) copy-start(f32[2,3,32,256]{3,2,1,0:T(8,128)} %param.29) | copy-start | bytes 589828
  232.8 2.0 copy-start.9
  232.8 2.0 copy-start.12
  232.8 2.0 copy-start.13
  233.8 2.7 %copy-start.1 = (f32[2,1152,32]{1,2,0:T(8,128)S(1)}, f32[2,1152,32]{1,2,0:T(8,128)}, u32[]{:S(2)}) copy-start(f32[2,1152,32]{1,2,0:T(8,128)} %param.25) | copy-start | bytes 884740
  233.8 2.7 %copy-start.5 = (f32[2,1152,32]{1,2,0:T(8,128)S(1)}, f32[2,1152,32]{1,2,0:T(8,128)}, u32[]{:S(2)}) copy-start(f32[2,1152,32]{1,2,0:T(8,128)} %param.34) | copy-start | bytes 884740
  233.8 2.7 %copy-start.6 = (f32[2,1152,32]{1,2,0:T(8,128)S(1)}, f32[2,1152,32]{1,2,0:T(8,128)}, u32[]{:S(2)}) copy-start(f32[2,1152,32]{1,2,0:T(8,128)} %param.35) | copy-start | bytes 884740
  236.5 1.2 copy-start.17
  236.5 1.2 copy-start.14
  236.5 1.2 copy-start.18
  236.6 1.2 copy-start.19
  236.6 3.0 %copy-start.15 = (f32[2,2,256]{2,1,0:T(2,128)S(1)}, f32[2,2,256]{2,1,0:T(2,128)}, u32[]{:S(2)}) copy-start(f32[2,2,256]{2,1,0:T(2,128)} %gain_ref.1) | copy-start | bytes 12292
  236.6 3.0 %copy-start.20 = (f32[2,2,256]{2,1,0:T(2,128)S(1)}, f32[2,2,256]{2,1,0:T(2,128)}, u32[]{:S(2)}) copy-start(f32[2,2,256]{2,1,0:T(2,128)} %param.38) | copy-start | bytes 12292
  236.6 3.0 %copy-start.21 = (f32[2,2,256]{2,1,0:T(2,128)S(1)}, f32[2,2,256]{2,1,0:T(2,128)}, u32[]{:S(2)}) copy-start(f32[2,2,256]{2,1,0:T(2,128)} %param.39) | copy-start | bytes 12292
  236.6 4.2 %copy-start.8 = (f32[256,256]{1,0:T(8,128)S(1)}, f32[256,256]{1,0:T(8,128)}, u32[]{:S(2)}) copy-start(f32[256,256]{1,0:T(8,128)} %get-tuple-element.162) | copy-start | bytes 786436
  236.6 4.9 %copy-start.7 = (f32[256,256]{1,0:T(8,128)S(1)}, f32[256,256]{1,0:T(8,128)}, u32[]{:S(2)}) copy-start(f32[256,256]{1,0:T(8,128)} %get-tuple-element.163) | copy-start | bytes 786436
  239.6 2.6 %copy-start.16 = (f32[2,2,256]{2,1,0:T(2,128)}, f32[2,2,256]{2,1,0:T(2,128)S(1)}, u32[]{:S(2)}) copy-start(f32[2,2,256]{2,1,0:T(2,128)S(1)} %reshape.59) | copy-start | bytes 12292

commit v4 on v3

--- a/solution.py
+++ b/solution.py
@@ -13,6 +13,7 @@
 BF = jnp.bfloat16
 F32 = jnp.float32
 SPAN = 384
+PACE = (-2, 0, 1, 3, 5, 6)
 
 
 def nn(a, b):
@@ -168,7 +169,7 @@
 
         if part_index == 0:
             for j in range(3):
-                put(at + j * ch, entry_ref[l, j])
+                put(at + (0, 2, 1)[j] * ch, entry_ref[l, j])
         elif part_index == 4:
             put(at + 4 * ch + 2 * ff, down_ref[l])
         else:
@@ -351,18 +352,21 @@
 
     def tick():
         t = fetched[0]
-        if t < len(fetches) + 5:
-            fetched[0] += 1
-            for k, fetch in enumerate(fetches):
-                if 0 <= t - k < 6:
-                    fetch.step()
+        fetched[0] += 1
+        for k, fetch in enumerate(fetches):
+            if fetch.stage == 0 and t >= k + PACE[0]:
+                fetch.step()
+        for k, fetch in enumerate(fetches):
+            if 0 < fetch.stage < 6 and t >= k + PACE[fetch.stage]:
+                fetch.step()
         for total in sums:
             if total.stage < 6:
                 total.step()
 
     def need(l, part_index):
-        while fetches[5 * l + part_index].stage < 6:
-            tick()
+        fetch = fetches[5 * l + part_index]
+        while fetch.stage < 6:
+            fetch.step()
 
     def ready(l, k, at, size):
         total = Sums(l, k, pl.ds(at, size))
@@ -508,7 +512,7 @@
         need(l, 0)
         full = rows[2 * l]
         bm = nn(full, weight(columns(base, 0, ch))) * scale
-        xm = nn(full, weight(columns(base, 2, ch))) * scale
+        xm = nn(full, weight(columns(base, 1, ch))) * scale
         bx = bm * xm
         ext[l, 8:] = bx
         tail = send(
@@ -516,7 +520,8 @@
         )
         bcx[l, 0] = bm
         bcx[l, 2] = xm
-        cm = nn(full, weight(columns(base, 1, ch))) * scale
+        tick()
+        cm = nn(full, weight(columns(base, 2, ch))) * scale
         bcx[l, 1] = cm
         tick()
         tail.wait_recv()
@@ -547,6 +552,7 @@
 
         for j in range(ff // SPAN):
             need(l, 1 + j)
+            tick()
             both = nn(rows[2 * l + 1], weight(columns(at_gate, j, 2 * SPAN))) * scale
             gates[l, :, j * 2 * SPAN : (j + 1) * 2 * SPAN] = both
             g, up_value = both[:, :SPAN], both[:, SPAN:]
@@ -619,12 +625,14 @@
             halo_recv.at[layers + l],
             (before, z),
         )
-        dproj[0, :, ch : 2 * ch] = (dy * conv[l]).astype(BF)
+        dproj[0, :, 2 * ch :] = (dy * conv[l]).astype(BF)
         for j in range(3):
-            small_ref[pl.ds(3 * l + j, 1), :] = jnp.sum(dz * ext[l, 6 + j : 6 + j + tokens], axis=0, keepdims=True)
+            small_ref[pl.ds(j * layers + l, 1), :] = jnp.sum(dz * ext[l, 6 + j : 6 + j + tokens], axis=0, keepdims=True)
         turn(ie + 1)
         weight_grad(l, 5, gated, l, 0, ch, 3 * ch)
-        ready(l, 5, 3 * ch, ch)
+        turn(2 * l, 2 * l)
+        weight_grad(l, 5, dproj, 0, 2 * ch, ch, 2 * ch)
+        ready(l, 5, 2 * ch, 2 * ch)
         tick()
         tail.wait_recv()
         last = dext[l, tokens:]
@@ -634,19 +642,23 @@
         db = (dbx * bcx[l, 2]).astype(BF)
         dx = (dbx * bcx[l, 0]).astype(BF)
         dproj[0, :, :ch] = db
-        dproj[0, :, 2 * ch :] = dx
-        dc = dproj[0, :, ch : 2 * ch].astype(F32)
+        dproj[0, :, ch : 2 * ch] = dx
+        dc = dproj[0, :, 2 * ch :].astype(F32)
         inner = row_sum(db.astype(F32) * bcx[l, 0] + dc * bcx[l, 1] + dx.astype(F32) * bcx[l, 2])
         total = Total(2 * layers + 2 * l, inner)
 
         def norm1_piece(who, base=base):
             return nt(dproj[0], weight_rows(who, columns(base, 0, 3 * ch)))
 
+        if l == 0:
+            weight_grad(l, 0, dproj, 0, 0, 2 * ch, 0)
+            ready(l, 0, 0, 2 * ch)
         scatter = Scatter(2 * layers + 2 * l + 1, norm1_piece)
-        turn(2 * l, 2 * l)
-        weight_grad(l, 0, dproj, 0, 0, 3 * ch, 0)
+        if l > 0:
+            weight_grad(l, 0, dproj, 0, 0, 2 * ch, 0)
+            ready(l, 0, 0, 2 * ch)
+        tick()
         scatter.pass_on()
-        ready(l, 0, 0, 3 * ch)
         tick()
         dn1 = scatter.finish()
         grad = dmid + norm_backward(2 * l, dn1, total.finish(), gain_ref[l, 0:1], 3 * layers + 2 * l)
@@ -748,21 +760,68 @@
     return (weight - rate * (update + decay * weight), first_new, second_new)
 
 
-def taken_apart(flat, layers, ch, ff):
-    per = 4 * ch + 3 * ff
-    entry, leave, gates, down = [], [], [], []
-    for l in range(layers):
-        b = l * per
-        entry.append(jnp.stack([flat[:, b + c * ch : b + (c + 1) * ch] for c in range(3)]))
-        leave.append(flat[:, b + 3 * ch : b + 4 * ch].T)
-        g = b + 4 * ch
-        halves = [
-            jnp.concatenate([flat[:, g + 2 * j + k : g + 2 * j + k + SPAN] for j in range(0, ff, SPAN)], axis=1)
-            for k in (0, SPAN)
+def update_kernel(cfg, *refs):
+    ch, ff = cfg
+    ins, outs = refs[:22], refs[22:]
+    flat, small, hidden, grad = ins[:4]
+    entry, leave, gates, down, kern, gain = ins[4:10]
+    moments = ins[10:]
+    outs[0][...] = hidden[...]
+    outs[1][...] = grad[...]
+    at_gate = 4 * ch
+    pieces = (
+        [(0, (0, c), flat[:, k * ch : (k + 1) * ch]) for c, k in enumerate((0, 2, 1))]
+        + [(1, (0,), flat[:, 3 * ch : 4 * ch])]
+        + [
+            (
+                2,
+                (0, k, slice(None), slice(j * SPAN, (j + 1) * SPAN)),
+                flat[:, at_gate + (2 * j + k) * SPAN : at_gate + (2 * j + k + 1) * SPAN],
+            )
+            for k in range(2)
+            for j in range(ff // SPAN)
         ]
-        gates.append(jnp.stack(halves))
-        down.append(flat[:, g + 2 * ff : g + 3 * ff].T)
-    return tuple(jnp.stack(v) for v in (entry, leave, gates, down))
+        + [(3, (0,), flat[:, at_gate + 2 * ff : at_gate + 3 * ff])]
+        + [(4, (j,), small[2 * j : 2 * j + 2]) for j in range(3)]
+        + [(5, (l,), small[6 + 2 * l : 8 + 2 * l]) for l in range(2)]
+    )
+    for n, where, value in pieces:
+        rate, decay = (0.01, 0.1) if n < 4 else (0.2, 0.0)
+        new = adamw(ins[4 + n][where], value, moments[2 * n][where], moments[2 * n + 1][where], rate, decay)
+        outs[2 + n][where] = value
+        outs[8 + n][where] = new[0]
+        outs[14 + 2 * n][where] = new[1]
+        outs[15 + 2 * n][where] = new[2]
+
+
+def run_update(flat, small, hidden, grad, params, moments):
+    layers, _, rows, ch = params[0].shape
+    ff = params[2].shape[3]
+    per = flat.shape[1] // layers
+
+    def whole(a):
+        return pl.BlockSpec(a.shape, lambda l, n=a.ndim: (0,) * n)
+
+    def layer(a):
+        return pl.BlockSpec((1, *a.shape[1:]), lambda l, n=a.ndim: (l,) + (0,) * (n - 1))
+
+    def spec(n, a):
+        return layer(a) if n < 4 else whole(a)
+
+    each = [spec(n, a) for n, a in enumerate(params)]
+    token = pl.BlockSpec((hidden.shape[0] // layers, hidden.shape[1]), lambda l: (l, 0))
+    twice = [e for e in each for _ in range(2)]
+    shapes = [jax.ShapeDtypeStruct(a.shape, F32) for a in params]
+    two = [e for e in shapes for _ in range(2)]
+    token_shape = jax.ShapeDtypeStruct(hidden.shape, F32)
+    return pl.pallas_call(
+        functools.partial(update_kernel, (ch, ff)),
+        grid=(layers,),
+        out_shape=(token_shape, token_shape, *shapes, *shapes, *two),
+        in_specs=[pl.BlockSpec((rows, per), lambda l: (0, l)), whole(small), token, token, *each, *twice],
+        out_specs=(token, token, *each, *each, *twice),
+        name="update",
+    )(flat, small, hidden, grad, *params, *moments)
 
 
 def per_device(
@@ -792,43 +851,35 @@
     seqs = lax.axis_size("seq")
     weights = (entry_weight, jnp.swapaxes(exit_weight, 1, 2), gate_up, jnp.swapaxes(down_weight, 1, 2))
     hidden, grad, summed, small = run_step(inputs, cotangent, weights, conv_kernel, norm_gain, seqs)
-    entry_grad, exit_grad, gate_grad, down_grad = taken_apart(summed, layers, ch, ff)
-    kernel_grad = small[: 3 * layers].reshape(layers, 3, ch)
-    gain_grad = small[3 * layers : 5 * layers].reshape(layers, 2, ch)
-    entry_u, entry_f, entry_s = adamw(entry_weight, entry_grad, entry_first, entry_second, 0.01, 0.1)
-    exit_u, exit_f, exit_s = adamw(exit_weight, exit_grad, exit_first, exit_second, 0.01, 0.1)
-    gate_u, gate_f, gate_s = adamw(gate_up, gate_grad, gate_first, gate_second, 0.01, 0.1)
-    down_u, down_f, down_s = adamw(down_weight, down_grad, down_first, down_second, 0.01, 0.1)
-    kernel_u, kernel_f, kernel_s = adamw(conv_kernel, kernel_grad, kernel_first, kernel_second, 0.2, 0.0)
-    gain_u, gain_f, gain_s = adamw(norm_gain, gain_grad, gain_first, gain_second, 0.2, 0.0)
-    return (
+    flip = lambda a: jnp.swapaxes(a, 1, 2)
+    spin = lambda a: jnp.swapaxes(a, 0, 1)
+    keep = lambda a: a
+    turns = (keep, flip, keep, flip, spin, keep)
+    params = (entry_weight, exit_weight, gate_up, down_weight, conv_kernel, norm_gain)
+    moments = (
+        entry_first,
+        entry_second,
+        exit_first,
+        exit_second,
+        gate_first,
+        gate_second,
+        down_first,
+        down_second,
+        kernel_first,
+        kernel_second,
+        gain_first,
+        gain_second,
+    )
+    twice = [t for t in turns for _ in range(2)]
+    done = run_update(
+        summed,
+        small,
         hidden,
         grad,
-        entry_grad,
-        exit_grad,
-        gate_grad,
-        down_grad,
-        kernel_grad,
-        gain_grad,
-        entry_u,
-        exit_u,
-        gate_u,
-        down_u,
-        kernel_u,
-        gain_u,
-        entry_f,
-        entry_s,
-        exit_f,
-        exit_s,
-        gate_f,
-        gate_s,
-        down_f,
-        down_s,
-        kernel_f,
-        kernel_s,
-        gain_f,
-        gain_s,
+        [t(a) for t, a in zip(turns, params)],
+        [t(a) for t, a in zip(twice, moments)],
     )
+    return tuple(t(a) for t, a in zip((keep, keep, *turns, *turns, *twice), done))
 
 
 def solution(mesh):

time: 244 us -> 221 us (0.906)
  local copies, waits for them, and re-layouts: 9.55 us -> 1.29 us
  Pallas kernels: 227 us -> 219 us
  other arithmetic: 4.99 us -> 0 us
    pallas_call x1, Pallas kernels: 227 us -> 214 us  [run_step(): pl.pallas_call(functools.partial(step_kernel, (layers, seqs, tokens, ch,...]
    unnamed x51 -> x1, local copies, waits for them, and re-layouts: 6.47 us -> 1.29 us
    sub x6 -> x0, other arithmetic: 4.88 us -> none  [adamw(): return (weight - rate * (update + decay * weight), first_new, second_new)]
    pallas_call x0 -> x1, Pallas kernels: none -> 4.76 us  [run_update(): pl.pallas_call(functools.partial(update_kernel, (ch, ff)), grid=(layers,)...]
where the time goes in v4:
time: 221 us
  Pallas kernels  219 us (99%)
    pallas_call x1, Pallas kernels, run_step(): pl.pallas_call(functools.partial(step_kernel, (layers, seqs, tokens, ch,...  214 us
    pallas_call x1, Pallas kernels, run_update(): pl.pallas_call(functools.partial(update_kernel, (ch, ff)), grid=(layers,)...  4.76 us

profile of v4, /device:TPU:0, one launch (start us, length us, event | category | flops | bytes accessed | tf_op | source)
XLA Modules:
  0.0 221.3 jit_solution(20856396456456038)
XLA Ops:
  0.7 1.3 copy.46.kern_ref
  2.0 214.4 %layers.1 = (f32[256,256]{1,0:T(8,128)}, f32[256,256]{1,0:T(8,128)}, f32[32,8960]{1,0:T(8,128)}, f32[16,256]{1,0:T(8,128)}) custom-call(f32[256,256]{1,0:T(8,128)} %x_ref.1, f32[256,256]{1,0:T(8,128)} %cot_ref.1, f32[2,3,32,256]{3,2,1,0:T(8,128)} %refs_4_.1, f32[2,32,256]{2,1,0:T(8,128)} %bitcast.25, f32[2,2,32,1152]{3,2,1,0:T(8,128)} %refs_6_.1, ...), custom_call_target="tpu_custom_call" | custom-call | tf_op jit(solution)/shard_map/layers/pallas_call | solution.py:699
  216.3 4.8 %update.1 = (f32[256,256]{1,0:T(8,128)}, f32[256,256]{1,0:T(8,128)}, f32[2,3,32,256]{3,2,1,0:T(8,128)}, f32[2,32,256]{2,1,0:T(8,128)}, f32[2,2,32,1152]{3,2,1,0:...) custom-call(f32[32,8960]{1,0:T(8,128)} %get-tuple-element.56.refs_0_, ...), custom_call_target="tpu_custom_call" | custom-call | tf_op jit(solution)/shard_map/update/pallas_call | solution.py:817

commit v5 on v4

--- a/solution.py
+++ b/solution.py
@@ -82,7 +82,6 @@
     credit,
 ):
     layers, seqs, tokens, ch, ff = cfg
-    half = tokens // 2
     width = 4 * ch
     per = 4 * ch + 3 * ff
     z = lax.axis_index("tp")
@@ -104,11 +103,13 @@
     up, un, uo = lax.rem(u + 3, 4), lax.rem(u + 1, 4), lax.rem(u + 2, 4)
     vp, vn, vo = lax.rem(v + 3, 4), lax.rem(v + 1, 4), lax.rem(v + 2, 4)
     u_next, u_prev, v_next, v_prev = device(un, v), device(up, v), device(u, vn), device(u, vp)
+    u_over, v_over = device(uo, v), device(u, vo)
     pair = (s + 1 - 2 * c, z)
 
     barrier = pltpu.get_barrier_semaphore()
     partners = [(s, zr), (s, zl), (s, zo), (after, z), (before, z), u_next, u_prev, v_next, v_prev, pair]
-    partners += [device(uo, v), device(u, vo)]
+    partners += [u_over, v_over]
+    partners += [(lax.rem(x + k, 4) * 8 + y * 2 + 1 - c, z) for k in (1, 2, 3)]
     for where in partners:
         pl.semaphore_signal(barrier, inc=1, device_id=where, device_id_type=MESH)
     pl.semaphore_wait(barrier, len(partners))
@@ -128,8 +129,6 @@
 
     def own_rows(who):
         return pl.ds(pl.multiple_of(who * ch, ch), ch)
-
-    top, low = pl.ds(0, half), pl.ds(half, half)
 
     def chunk_of(ref, lead, vv, lo, hi, where):
         if lead == 0:
@@ -200,9 +199,33 @@
 
             return send_either(make, w_send.at[self.k, n], w_recv.at[self.k, n], where)
 
+        def direct(self, stage):
+            if stage == 0:
+                pack(self.k)
+                self.got = [
+                    self.move(self.block(u, v), n, where) for n, where in enumerate((u_over, u_next, u_prev))
+                ]
+            elif stage == 1:
+                for copy in self.got:
+                    copy.wait_recv()
+                self.got = [
+                    self.move_row(v, 0, 4, 4 + n, where) for n, where in enumerate((v_over, v_next, v_prev))
+                ]
+                self.p0 = self.move_row(v, 0, 4, 8, pair)
+            elif stage == 2:
+                for n, (copy, vv) in enumerate(zip(self.got[::-1], (vn, vp, vo))):
+                    copy.wait_recv()
+                    self.got[2 - n] = self.move_row(vv, 0, 4, 9 + n, pair)
+            else:
+                for copy in (self.p0, *self.got):
+                    copy.wait_recv()
+                self.stage = 6
+
         def step(self):
             stage, self.stage = self.stage, self.stage + 1
-            if stage == 0:
+            if self.k == 0:
+                self.direct(stage)
+            elif stage == 0:
                 pack(self.k)
                 self.a0 = self.move(self.block(u, v), 0, u_next)
                 self.a1 = self.move(self.block(u, v), 1, u_prev)
@@ -287,23 +310,56 @@
             if not self.first:
                 pl.semaphore_wait(credit.at[self.k, kind], count)
 
+        def add_pair(self):
+            self.q.wait_recv()
+
+            @pl.loop(0, 4)
+            def _(i):
+                gw_ref[i, :, c, :, self.where] = (
+                    gw_ref[i, :, c, :, self.where].astype(F32) + from_pair[i, :, :, self.where].astype(F32)
+                ).astype(BF)
+
+        def direct(self, stage, upper, lower):
+            if stage == 1:
+                self.add_pair()
+                self.ask(1, 3)
+                pairs = ((vo, v_over), (vn, v_next), (vp, v_prev))
+                self.got = [
+                    self.far(vv, 2 * k, 1 + 2 * n + k, where) for n, (vv, where) in enumerate(pairs) for k in (0, 1)
+                ]
+            elif stage == 2:
+                for copy in self.got:
+                    copy.wait_recv()
+                self.add_far(v, 0, [0, 2, 4])
+                self.add_far(v, 2, [1, 3, 5])
+                self.ask(2, 3)
+                pairs = ((uo, u_over), (un, u_next), (up, u_prev))
+                self.got = [
+                    self.near(uu, r, 7 + 2 * n + k, where)
+                    for n, (uu, where) in enumerate(pairs)
+                    for k, r in enumerate((upper, lower))
+                ]
+            else:
+                for copy in self.got:
+                    copy.wait_recv()
+                final_ref[0:16, self.total] = self.add_near(u, upper, [0, 2, 4])
+                final_ref[16:32, self.total] = self.add_near(u, lower, [1, 3, 5])
+                for copy in self.sent:
+                    copy.wait_send()
+                self.stage = 6
+
         def step(self):
             stage, self.stage = self.stage, self.stage + 1
             upper, lower = pl.ds(0, 16), pl.ds(16, 16)
-            if stage == 0:
+            if self.l == 0 and self.k == 0 and stage > 0:
+                self.direct(stage, upper, lower)
+            elif stage == 0:
                 self.ask(0, 1)
                 self.q = self.send(
                     gw_ref.at[:, :, 1 - c, :, self.where], from_pair.at[:, :, :, self.where], 0, pair
                 )
             elif stage == 1:
-                self.q.wait_recv()
-
-                @pl.loop(0, 4)
-                def _(i):
-                    gw_ref[i, :, c, :, self.where] = (
-                        gw_ref[i, :, c, :, self.where].astype(F32) + from_pair[i, :, :, self.where].astype(F32)
-                    ).astype(BF)
-
+                self.add_pair()
                 self.allow(0, [pair])
                 self.ask(1, 2)
                 self.f0 = self.far(vo, 0, 1, v_next)
@@ -322,7 +378,7 @@
                     copy.wait_recv()
                 self.add_far(v, 0, [3, 4])
                 self.add_far(v, 2, [2, 5])
-                self.allow(1, [v_next, v_prev])
+                self.allow(1, [v_next, v_prev, v_over] if self.k == 0 else [v_next, v_prev])
                 self.ask(2, 2)
                 self.n0 = self.near(uo, upper, 7, u_next)
                 self.n1 = self.near(uo, lower, 8, u_prev)
@@ -342,7 +398,7 @@
                     copy.wait_recv()
                 final_ref[0:16, self.total] = self.add_near(u, upper, [3, 4])
                 final_ref[16:32, self.total] = self.add_near(u, lower, [2, 5])
-                self.allow(2, [u_next, u_prev])
+                self.allow(2, [u_next, u_prev, u_over] if self.k == 0 else [u_next, u_prev])
                 for copy in self.sent:
                     copy.wait_send()
 
@@ -389,63 +445,30 @@
 
     class Gather:
         def __init__(self, i, block):
-            self.i = i
             rows[i, :, cols(z)] = block
-            mine = lambda r: rows.at[i, r, cols(z)]
-            self.r1 = send(mine(top), mine(top), ag_send.at[i, 0], ag_recv.at[i, 0], (s, zr))
-            self.l1 = send(mine(low), mine(low), ag_send.at[i, 1], ag_recv.at[i, 1], (s, zl))
-            self.r2 = send(mine(low), mine(low), ag_send.at[i, 2], ag_recv.at[i, 2], (s, zr))
-            self.l2 = send(mine(top), mine(top), ag_send.at[i, 3], ag_recv.at[i, 3], (s, zl))
-
-        def pass_on(self):
-            i = self.i
-            self.r1.wait_recv()
-            b = rows.at[i, top, cols(zl)]
-            self.rf = send(b, b, ag_send.at[i, 4], ag_recv.at[i, 4], (s, zr))
-            self.l1.wait_recv()
-            b = rows.at[i, low, cols(zr)]
-            self.lf = send(b, b, ag_send.at[i, 5], ag_recv.at[i, 5], (s, zl))
+            mine = rows.at[i, :, cols(z)]
+            self.got = [
+                send(mine, mine, ag_send.at[i, k], ag_recv.at[i, k], (s, who)) for k, who in enumerate((zo, zr, zl))
+            ]
 
         def finish(self):
-            for c in (self.r2, self.l2, self.rf, self.lf):
-                c.wait_recv()
+            for copy in self.got:
+                copy.wait_recv()
 
     class Scatter:
         def __init__(self, i, piece):
-            self.i = i
-            at = lambda k, r: stage.at[i, k, r]
-            to = lambda k: landed.at[i, k]
-            stage[i, 0] = piece(zo).astype(BF)
-            self.r1 = send(at(0, top), to(0), rs_send.at[i, 0], rs_recv.at[i, 0], (s, zr))
-            self.l1 = send(at(0, low), to(1), rs_send.at[i, 1], rs_recv.at[i, 1], (s, zl))
-            right = piece(zr)
-            stage[i, 1, half:] = right[half:].astype(BF)
-            self.r2 = send(at(1, low), to(2), rs_send.at[i, 2], rs_recv.at[i, 2], (s, zr))
-            part[0] = right[:half]
-            left = piece(zl)
-            stage[i, 2, :half] = left[:half].astype(BF)
-            self.l2 = send(at(2, top), to(3), rs_send.at[i, 3], rs_recv.at[i, 3], (s, zl))
-            part[1] = left[half:]
-            own = piece(z)
-            part[2] = own[:half]
-            part[3] = own[half:]
-
-        def pass_on(self):
+            self.i, self.got = i, []
+            for k, who in enumerate((zo, zr, zl)):
+                stage[i, k] = piece(who).astype(BF)
+                copy = send(stage.at[i, k], landed.at[i, k], rs_send.at[i, k], rs_recv.at[i, k], (s, who))
+                self.got.append(copy)
+            part[...] = piece(z)
+
+        def finish(self):
+            for copy in self.got:
+                copy.wait_recv()
             i = self.i
-            self.r1.wait_recv()
-            stage[i, 1, :half] = (part[0] + landed[i, 0].astype(F32)).astype(BF)
-            self.rf = send(stage.at[i, 1, top], landed.at[i, 4], rs_send.at[i, 4], rs_recv.at[i, 4], (s, zr))
-            self.l1.wait_recv()
-            stage[i, 2, half:] = (part[1] + landed[i, 1].astype(F32)).astype(BF)
-            self.lf = send(stage.at[i, 2, low], landed.at[i, 5], rs_send.at[i, 5], rs_recv.at[i, 5], (s, zl))
-
-        def finish(self):
-            i = self.i
-            for c in (self.r2, self.l2, self.rf, self.lf):
-                c.wait_recv()
-            upper = part[2] + landed[i, 4].astype(F32) + landed[i, 3].astype(F32)
-            lower = part[3] + landed[i, 2].astype(F32) + landed[i, 5].astype(F32)
-            return jnp.concatenate([upper, lower], axis=0)
+            return part[...] + landed[i, 0].astype(F32) + landed[i, 1].astype(F32) + landed[i, 2].astype(F32)
 
     class Total:
         def __init__(self, i, sums):
@@ -503,11 +526,8 @@
         if l == 0:
             cot_gather = Gather(2 * layers + 2 * (layers - 1), cot_ref[...].astype(BF))
         tick()
-        gather.pass_on()
         tick()
         gather.finish()
-        if l == 0:
-            cot_gather.pass_on()
         scale = norm_scale(2 * l, total, hidden)
         need(l, 0)
         full = rows[2 * l]
@@ -527,8 +547,8 @@
         tail.wait_recv()
         head = ext[l, 0:8]
         ext[l, 0:8] = jnp.where(s > 0, head, jnp.zeros_like(head))
-        k = kern_ref[l]
-        zc = k[0:1] * ext[l, 6 : 6 + tokens] + k[1:2] * ext[l, 7 : 7 + tokens] + k[2:3] * ext[l, 8 : 8 + tokens]
+        k = [kern_ref[j, l : l + 1] for j in range(3)]
+        zc = k[0] * ext[l, 6 : 6 + tokens] + k[1] * ext[l, 7 : 7 + tokens] + k[2] * ext[l, 8 : 8 + tokens]
         conv[l] = zc
         gated[l] = (cm * zc).astype(BF)
 
@@ -538,13 +558,11 @@
         need(l, 1)
         scatter = Scatter(2 * l, exit_piece)
         tick()
-        scatter.pass_on()
         tick()
         mid = hidden + scatter.finish()
         gather = Gather(2 * l + 1, (mid * gain_ref[l, 1:2]).astype(BF))
         total = Total(2 * l + 1, row_sum(mid * mid))
         tick()
-        gather.pass_on()
         tick()
         gather.finish()
         scale = norm_scale(2 * l + 1, total, mid)
@@ -564,7 +582,6 @@
         need(l, 4)
         scatter = Scatter(2 * l + 1, down_piece)
         tick()
-        scatter.pass_on()
         tick()
         hidden = mid + scatter.finish()
     out_ref[...] = hidden
@@ -579,7 +596,6 @@
         else:
             gather = Gather(ie, grad.astype(BF))
             tick()
-            gather.pass_on()
             tick()
         gather.finish()
 
@@ -602,7 +618,6 @@
         scatter = Scatter(2 * layers + 2 * l, norm2_piece)
         turn(ie)
         weight_grad(l, 4, acted, l, 0, ff, 4 * ch + 2 * ff)
-        scatter.pass_on()
         ready(l, 4, 4 * ch + 2 * ff, ff)
         turn(2 * l + 1, 2 * l + 1)
         for j in range(ff // SPAN):
@@ -612,7 +627,6 @@
         dmid = grad + norm_backward(2 * l + 1, dn2, total.finish(), gain_ref[l, 1:2], 3 * layers + 2 * l + 1)
         gather = Gather(ie + 1, dmid.astype(BF))
         tick()
-        gather.pass_on()
         tick()
         gather.finish()
         dy = nn(rows[ie + 1], weight(columns(at_exit, 0, ch)))
@@ -637,8 +651,8 @@
         tail.wait_recv()
         last = dext[l, tokens:]
         dext[l, tokens:] = jnp.where(s < seqs - 1, last, jnp.zeros_like(last))
-        k = kern_ref[l]
-        dbx = k[2:3] * dext[l, 0:tokens] + k[1:2] * dext[l, 1 : 1 + tokens] + k[0:1] * dext[l, 2 : 2 + tokens]
+        k = [kern_ref[j, l : l + 1] for j in range(3)]
+        dbx = k[2] * dext[l, 0:tokens] + k[1] * dext[l, 1 : 1 + tokens] + k[0] * dext[l, 2 : 2 + tokens]
         db = (dbx * bcx[l, 2]).astype(BF)
         dx = (dbx * bcx[l, 0]).astype(BF)
         dproj[0, :, :ch] = db
@@ -658,29 +672,26 @@
             weight_grad(l, 0, dproj, 0, 0, 2 * ch, 0)
             ready(l, 0, 0, 2 * ch)
         tick()
-        scatter.pass_on()
         tick()
         dn1 = scatter.finish()
         grad = dmid + norm_backward(2 * l, dn1, total.finish(), gain_ref[l, 0:1], 3 * layers + 2 * l)
     din_ref[...] = grad
-    own = tally.at[0, 0]
-    tally[0, 0] = small_ref[...]
-    copy = send(own, tally.at[0, 1], t_send.at[0], t_recv.at[0], pair)
+    tally[0, 2 * x + c] = small_ref[...]
+    slot = tally.at[0, 2 * x + c]
+    near_by = [(lax.rem(x + k // 2, 4) * 8 + y * 2 + lax.rem(c + k, 2), z) for k in range(1, 8)]
+    copies = [send(slot, slot, t_send.at[k], t_recv.at[k], where) for k, where in enumerate(near_by)]
     tick()
-    copy.wait_recv()
-    tally[1, x] = tally[0, 0] + tally[0, 1]
-    stages = ((1, x, lambda k: (lax.rem(x + k, 4) * 8 + y * 2 + c, z)), (2, y, lambda k: (x * 8 + lax.rem(y + k, 4) * 2 + c, z)))
-    for n, here, where in stages:
-        slot = tally.at[n, here]
-        copies = [send(slot, slot, t_send.at[3 * n - 3 + k], t_recv.at[3 * n - 3 + k], where(k)) for k in (1, 2, 3)]
-        tick()
-        for copy in copies:
-            copy.wait_recv()
-        total = tally[n, 0] + tally[n, 1] + tally[n, 2] + tally[n, 3]
-        if n == 1:
-            tally[2, y] = total
-        else:
-            small_ref[...] = total
+    for copy in copies:
+        copy.wait_recv()
+    tally[1, y] = sum((tally[0, k] for k in range(1, 8)), tally[0, 0])
+    slot = tally.at[1, y]
+    copies = [
+        send(slot, slot, t_send.at[6 + k], t_recv.at[6 + k], (x * 8 + lax.rem(y + k, 4) * 2 + c, z)) for k in (1, 2, 3)
+    ]
+    tick()
+    for copy in copies:
+        copy.wait_recv()
+    small_ref[...] = tally[1, 0] + tally[1, 1] + tally[1, 2] + tally[1, 3]
     while any(total.stage < 6 for total in sums):
         tick()
     for copy in pending:
@@ -688,7 +699,7 @@
 
 
 def run_step(x, cot, weights, kern, gain, seqs):
-    layers, taps, ch = kern.shape
+    taps, layers, ch = kern.shape
     tokens = x.shape[0]
     width = 4 * ch
     ff = weights[2].shape[3]
@@ -708,9 +719,9 @@
         out_specs=(vmem,) * 4,
         scratch_shapes=[
             pltpu.VMEM((n, tokens, width), BF),
-            pltpu.VMEM((4, tokens // 2, ch), F32),
+            pltpu.VMEM((tokens, ch), F32),
             pltpu.VMEM((n, 3, tokens, ch), BF),
-            pltpu.VMEM((n, 6, tokens // 2, ch), BF),
+            pltpu.VMEM((n, 3, tokens, ch), BF),
             pltpu.VMEM((n, 4, 8, tokens), F32),
             pltpu.VMEM((2 * layers, tokens, ch), F32),
             pltpu.VMEM((2 * layers, tokens, 128), F32),
@@ -729,11 +740,11 @@
             pltpu.VMEM((4, 4, 32, per), BF),
             pltpu.VMEM((6, 2, 32, per), BF),
             pltpu.VMEM((6, 16, per), BF),
-            pltpu.VMEM((3, 4, 16, ch), F32),
-            dma((n, 6)),
-            dma((n, 6)),
-            dma((n, 6)),
-            dma((n, 6)),
+            pltpu.VMEM((2, 8, 16, ch), F32),
+            dma((n, 3)),
+            dma((n, 3)),
+            dma((n, 3)),
+            dma((n, 3)),
             dma((n, 3)),
             dma((n, 3)),
             dma((2 * layers,)),
@@ -742,8 +753,8 @@
             dma((5 * layers, 12)),
             dma((layers, 6, 13)),
             dma((layers, 6, 13)),
-            dma((7,)),
-            dma((7,)),
+            dma((10,)),
+            dma((10,)),
             pltpu.SemaphoreType.REGULAR((6, 3)),
         ],
         compiler_params=pltpu.CompilerParams(
@@ -850,7 +861,7 @@
     ff = gate_up.shape[3]
     seqs = lax.axis_size("seq")
     weights = (entry_weight, jnp.swapaxes(exit_weight, 1, 2), gate_up, jnp.swapaxes(down_weight, 1, 2))
-    hidden, grad, summed, small = run_step(inputs, cotangent, weights, conv_kernel, norm_gain, seqs)
+    hidden, grad, summed, small = run_step(inputs, cotangent, weights, jnp.swapaxes(conv_kernel, 0, 1), norm_gain, seqs)
     flip = lambda a: jnp.swapaxes(a, 1, 2)
     spin = lambda a: jnp.swapaxes(a, 0, 1)
     keep = lambda a: a

time: 221 us -> 219 us (level)
  no operation moved by 1% of the time
where the time goes in v5:
time: 219 us
  Pallas kernels  218 us (100%)
    pallas_call x1, Pallas kernels, run_step(): pl.pallas_call(functools.partial(step_kernel, (layers, seqs, tokens, ch,...  213 us
    pallas_call x1, Pallas kernels, run_update(): pl.pallas_call(functools.partial(update_kernel, (ch, ff)), grid=(layers,)...  4.76 us

profile of v5, /device:TPU:0, one launch (start us, length us, event | category | flops | bytes accessed | tf_op | source)
XLA Modules:
  0.0 218.7 jit_solution(5405804071358731643)
XLA Ops:
  0.7 213.1 %layers.1 = (f32[256,256]{1,0:T(8,128)}, f32[256,256]{1,0:T(8,128)}, f32[32,8960]{1,0:T(8,128)}, f32[16,256]{1,0:T(8,128)}) custom-call(f32[256,256]{1,0:T(8,128)} %x_ref.1, f32[256,256]{1,0:T(8,128)} %cot_ref.1, f32[2,3,32,256]{3,2,1,0:T(8,128)} %refs_4_.1, f32[2,32,256]{2,1,0:T(8,128)} %bitcast.25, f32[2,2,32,1152]{3,2,1,0:T(8,128)} %refs_6_.1, ...), custom_call_target="tpu_custom_call" | custom-call | tf_op jit(solution)/shard_map/layers/pallas_call | solution.py:710
  213.8 4.8 %update.1 = (f32[256,256]{1,0:T(8,128)}, f32[256,256]{1,0:T(8,128)}, f32[2,3,32,256]{3,2,1,0:T(8,128)}, f32[2,32,256]{2,1,0:T(8,128)}, f32[2,2,32,1152]{3,2,1,0:...) custom-call(f32[32,8960]{1,0:T(8,128)} %get-tuple-element.56.refs_0_, ...), custom_call_target="tpu_custom_call" | custom-call | tf_op jit(solution)/shard_map/update/pallas_call | solution.py:828

commit v6 on v5

--- a/solution.py
+++ b/solution.py
@@ -223,7 +223,7 @@
 
         def step(self):
             stage, self.stage = self.stage, self.stage + 1
-            if self.k == 0:
+            if self.k < 2:
                 self.direct(stage)
             elif stage == 0:
                 pack(self.k)
@@ -260,6 +260,7 @@
             self.l, self.k, self.where, self.stage = l, k, where, 0
             self.total = pl.ds(l * per + where.start, where.size)
             self.first = l == layers - 1
+            self.due = 0
             self.sent = []
 
         def send(self, src, dst, n, where):
@@ -416,7 +417,8 @@
             if 0 < fetch.stage < 6 and t >= k + PACE[fetch.stage]:
                 fetch.step()
         for total in sums:
-            if total.stage < 6:
+            if total.stage < 6 and (t >= total.due or total.l + total.k == 0):
+                total.due = t + 2
                 total.step()
 
     def need(l, part_index):
@@ -456,13 +458,17 @@
                 copy.wait_recv()
 
     class Scatter:
-        def __init__(self, i, piece):
-            self.i, self.got = i, []
+        def __init__(self, i, piece, lo=0, hi=tokens):
+            self.i, self.piece, self.got = i, piece, []
+            self.give(lo, hi, 0)
+
+        def give(self, lo, hi, at):
+            i = self.i
             for k, who in enumerate((zo, zr, zl)):
-                stage[i, k] = piece(who).astype(BF)
-                copy = send(stage.at[i, k], landed.at[i, k], rs_send.at[i, k], rs_recv.at[i, k], (s, who))
-                self.got.append(copy)
-            part[...] = piece(z)
+                stage[i, k, lo:hi] = self.piece(who, lo, hi).astype(BF)
+                here, there = stage.at[i, k, pl.ds(lo, hi - lo)], landed.at[i, k, pl.ds(lo, hi - lo)]
+                self.got.append(send(here, there, rs_send.at[i, at + k], rs_recv.at[i, at + k], (s, who)))
+            part[lo:hi] = self.piece(z, lo, hi)
 
         def finish(self):
             for copy in self.got:
@@ -543,20 +549,24 @@
         tick()
         cm = nn(full, weight(columns(base, 2, ch))) * scale
         bcx[l, 1] = cm
-        tick()
+        k = [kern_ref[j, l : l + 1] for j in range(3)]
+
+        def mix(lo, hi, l=l, k=k):
+            zc = sum(k[j] * ext[l, 6 + j + lo : 6 + j + hi] for j in range(3))
+            conv[l, lo:hi] = zc
+            gated[l, lo:hi] = (bcx[l, 1, lo:hi] * zc).astype(BF)
+
+        def exit_piece(who, lo, hi, l=l, at=at_exit):
+            return nt(gated[l, lo:hi], weight_rows(who, columns(at, 0, ch)))
+
+        mix(16, tokens)
+        need(l, 1)
+        scatter = Scatter(2 * l, exit_piece, 16)
         tail.wait_recv()
         head = ext[l, 0:8]
         ext[l, 0:8] = jnp.where(s > 0, head, jnp.zeros_like(head))
-        k = [kern_ref[j, l : l + 1] for j in range(3)]
-        zc = k[0] * ext[l, 6 : 6 + tokens] + k[1] * ext[l, 7 : 7 + tokens] + k[2] * ext[l, 8 : 8 + tokens]
-        conv[l] = zc
-        gated[l] = (cm * zc).astype(BF)
-
-        def exit_piece(who, l=l, at=at_exit):
-            return nt(gated[l], weight_rows(who, columns(at, 0, ch)))
-
-        need(l, 1)
-        scatter = Scatter(2 * l, exit_piece)
+        mix(0, 16)
+        scatter.give(0, 16, 3)
         tick()
         tick()
         mid = hidden + scatter.finish()
@@ -576,7 +586,7 @@
             g, up_value = both[:, :SPAN], both[:, SPAN:]
             acted[l, :, j * SPAN : (j + 1) * SPAN] = (g * jax.nn.sigmoid(g) * up_value).astype(BF)
 
-        def down_piece(who, l=l, at=at_down):
+        def down_piece(who, lo, hi, l=l, at=at_down):
             return nt(acted[l], weight_rows(who, columns(at, 0, ff)))
 
         need(l, 4)
@@ -612,7 +622,7 @@
             inner += row_sum(dg.astype(F32) * g + du.astype(F32) * up_value)
         total = Total(2 * layers + 2 * l + 1, inner)
 
-        def norm2_piece(who, at_gate=at_gate):
+        def norm2_piece(who, lo, hi, at_gate=at_gate):
             return nt(dgates[0], weight_rows(who, columns(at_gate, 0, 2 * ff)))
 
         scatter = Scatter(2 * layers + 2 * l, norm2_piece)
@@ -640,34 +650,43 @@
             (before, z),
         )
         dproj[0, :, 2 * ch :] = (dy * conv[l]).astype(BF)
-        for j in range(3):
-            small_ref[pl.ds(j * layers + l, 1), :] = jnp.sum(dz * ext[l, 6 + j : 6 + j + tokens], axis=0, keepdims=True)
+        k = [kern_ref[j, l : l + 1] for j in range(3)]
+
+        def unmix(lo, hi, l=l, k=k):
+            dbx = sum(k[2 - j] * dext[l, lo + j : hi + j] for j in range(3))
+            db = (dbx * bcx[l, 2, lo:hi]).astype(BF)
+            dx = (dbx * bcx[l, 0, lo:hi]).astype(BF)
+            dproj[0, lo:hi, :ch] = db
+            dproj[0, lo:hi, ch : 2 * ch] = dx
+            dc = dproj[0, lo:hi, 2 * ch :].astype(F32)
+            return row_sum(
+                db.astype(F32) * bcx[l, 0, lo:hi] + dc * bcx[l, 1, lo:hi] + dx.astype(F32) * bcx[l, 2, lo:hi]
+            )
+
+        def norm1_piece(who, lo, hi, base=base):
+            return nt(dproj[0, lo:hi], weight_rows(who, columns(base, 0, 3 * ch)))
+
+        late = tokens - 16
+        inner = unmix(0, late)
+        scatter = Scatter(2 * layers + 2 * l + 1, norm1_piece, 0, late)
         turn(ie + 1)
         weight_grad(l, 5, gated, l, 0, ch, 3 * ch)
-        turn(2 * l, 2 * l)
-        weight_grad(l, 5, dproj, 0, 2 * ch, ch, 2 * ch)
-        ready(l, 5, 2 * ch, 2 * ch)
-        tick()
         tail.wait_recv()
         last = dext[l, tokens:]
         dext[l, tokens:] = jnp.where(s < seqs - 1, last, jnp.zeros_like(last))
-        k = [kern_ref[j, l : l + 1] for j in range(3)]
-        dbx = k[2] * dext[l, 0:tokens] + k[1] * dext[l, 1 : 1 + tokens] + k[0] * dext[l, 2 : 2 + tokens]
-        db = (dbx * bcx[l, 2]).astype(BF)
-        dx = (dbx * bcx[l, 0]).astype(BF)
-        dproj[0, :, :ch] = db
-        dproj[0, :, ch : 2 * ch] = dx
-        dc = dproj[0, :, 2 * ch :].astype(F32)
-        inner = row_sum(db.astype(F32) * bcx[l, 0] + dc * bcx[l, 1] + dx.astype(F32) * bcx[l, 2])
+        inner = jnp.concatenate([inner, unmix(late, tokens)], axis=0)
         total = Total(2 * layers + 2 * l, inner)
-
-        def norm1_piece(who, base=base):
-            return nt(dproj[0], weight_rows(who, columns(base, 0, 3 * ch)))
-
+        scatter.give(late, tokens, 3)
+        for j in range(3):
+            small_ref[pl.ds(j * layers + l, 1), :] = jnp.sum(
+                dz * ext[l, 6 + j : 6 + j + tokens], axis=0, keepdims=True
+            )
+        turn(2 * l, 2 * l)
         if l == 0:
             weight_grad(l, 0, dproj, 0, 0, 2 * ch, 0)
             ready(l, 0, 0, 2 * ch)
-        scatter = Scatter(2 * layers + 2 * l + 1, norm1_piece)
+        weight_grad(l, 5, dproj, 0, 2 * ch, ch, 2 * ch)
+        ready(l, 5, 2 * ch, 2 * ch)
         if l > 0:
             weight_grad(l, 0, dproj, 0, 0, 2 * ch, 0)
             ready(l, 0, 0, 2 * ch)
@@ -743,8 +762,8 @@
             pltpu.VMEM((2, 8, 16, ch), F32),
             dma((n, 3)),
             dma((n, 3)),
-            dma((n, 3)),
-            dma((n, 3)),
+            dma((n, 6)),
+            dma((n, 6)),
             dma((n, 3)),
             dma((n, 3)),
             dma((2 * layers,)),

time: 219 us -> 201 us (0.918)
  Pallas kernels: 218 us -> 200 us
    pallas_call x1, Pallas kernels: 213 us -> 195 us  [run_step(): pl.pallas_call(functools.partial(step_kernel, (layers, seqs, tokens, ch,...]
where the time goes in v6:
time: 201 us
  Pallas kernels  200 us (100%)
    pallas_call x1, Pallas kernels, run_step(): pl.pallas_call(functools.partial(step_kernel, (layers, seqs, tokens, ch,...  195 us
    pallas_call x1, Pallas kernels, run_update(): pl.pallas_call(functools.partial(update_kernel, (ch, ff)), grid=(layers,)...  4.76 us

profile of v6, /device:TPU:0, one launch (start us, length us, event | category | flops | bytes accessed | tf_op | source)
XLA Modules:
  0.0 200.9 jit_solution(15023971078958006498)
XLA Ops:
  0.7 195.2 %layers.1 = (f32[256,256]{1,0:T(8,128)}, f32[256,256]{1,0:T(8,128)}, f32[32,8960]{1,0:T(8,128)}, f32[16,256]{1,0:T(8,128)}) custom-call(f32[256,256]{1,0:T(8,128)} %x_ref.1, f32[256,256]{1,0:T(8,128)} %cot_ref.1, f32[2,3,32,256]{3,2,1,0:T(8,128)} %refs_4_.1, f32[2,32,256]{2,1,0:T(8,128)} %bitcast.25, f32[2,2,32,1152]{3,2,1,0:T(8,128)} %refs_6_.1, ...), custom_call_target="tpu_custom_call" | custom-call | tf_op jit(solution)/shard_map/layers/pallas_call | solution.py:729
  195.9 4.8 %update.1 = (f32[256,256]{1,0:T(8,128)}, f32[256,256]{1,0:T(8,128)}, f32[2,3,32,256]{3,2,1,0:T(8,128)}, f32[2,32,256]{2,1,0:T(8,128)}, f32[2,2,32,1152]{3,2,1,0:...) custom-call(f32[32,8960]{1,0:T(8,128)} %get-tuple-element.56.refs_0_, ...), custom_call_target="tpu_custom_call" | custom-call | tf_op jit(solution)/shard_map/update/pallas_call | solution.py:847

commit v7 on v6

--- a/solution.py
+++ b/solution.py
@@ -352,7 +352,7 @@
         def step(self):
             stage, self.stage = self.stage, self.stage + 1
             upper, lower = pl.ds(0, 16), pl.ds(16, 16)
-            if self.l == 0 and self.k == 0 and stage > 0:
+            if self.l == 0 and self.k in (0, 5) and stage > 0:
                 self.direct(stage, upper, lower)
             elif stage == 0:
                 self.ask(0, 1)
@@ -379,7 +379,7 @@
                     copy.wait_recv()
                 self.add_far(v, 0, [3, 4])
                 self.add_far(v, 2, [2, 5])
-                self.allow(1, [v_next, v_prev, v_over] if self.k == 0 else [v_next, v_prev])
+                self.allow(1, [v_next, v_prev, v_over] if self.k in (0, 5) else [v_next, v_prev])
                 self.ask(2, 2)
                 self.n0 = self.near(uo, upper, 7, u_next)
                 self.n1 = self.near(uo, lower, 8, u_prev)
@@ -399,7 +399,7 @@
                     copy.wait_recv()
                 final_ref[0:16, self.total] = self.add_near(u, upper, [3, 4])
                 final_ref[16:32, self.total] = self.add_near(u, lower, [2, 5])
-                self.allow(2, [u_next, u_prev, u_over] if self.k == 0 else [u_next, u_prev])
+                self.allow(2, [u_next, u_prev, u_over] if self.k in (0, 5) else [u_next, u_prev])
                 for copy in self.sent:
                     copy.wait_send()
 
@@ -417,7 +417,7 @@
             if 0 < fetch.stage < 6 and t >= k + PACE[fetch.stage]:
                 fetch.step()
         for total in sums:
-            if total.stage < 6 and (t >= total.due or total.l + total.k == 0):
+            if total.stage < 6 and (t >= total.due or (total.l == 0 and total.k in (0, 5))):
                 total.due = t + 2
                 total.step()
 

time: 201 us -> 201 us (level)
  no operation moved by 1% of the time
where the time goes in v7:
time: 201 us
  Pallas kernels  200 us (100%)
    pallas_call x1, Pallas kernels, run_step(): pl.pallas_call(functools.partial(step_kernel, (layers, seqs, tokens, ch,...  195 us
    pallas_call x1, Pallas kernels, run_update(): pl.pallas_call(functools.partial(update_kernel, (ch, ff)), grid=(layers,)...  4.76 us

profile of v7, /device:TPU:0, one launch (start us, length us, event | category | flops | bytes accessed | tf_op | source)
XLA Modules:
  0.0 200.8 jit_solution(4045709299695029842)
XLA Ops:
  0.7 195.2 %layers.1 = (f32[256,256]{1,0:T(8,128)}, f32[256,256]{1,0:T(8,128)}, f32[32,8960]{1,0:T(8,128)}, f32[16,256]{1,0:T(8,128)}) custom-call(f32[256,256]{1,0:T(8,128)} %x_ref.1, f32[256,256]{1,0:T(8,128)} %cot_ref.1, f32[2,3,32,256]{3,2,1,0:T(8,128)} %refs_4_.1, f32[2,32,256]{2,1,0:T(8,128)} %bitcast.25, f32[2,2,32,1152]{3,2,1,0:T(8,128)} %refs_6_.1, ...), custom_call_target="tpu_custom_call" | custom-call | tf_op jit(solution)/shard_map/layers/pallas_call | solution.py:729
  195.9 4.8 %update.1 = (f32[256,256]{1,0:T(8,128)}, f32[256,256]{1,0:T(8,128)}, f32[2,3,32,256]{3,2,1,0:T(8,128)}, f32[2,32,256]{2,1,0:T(8,128)}, f32[2,2,32,1152]{3,2,1,0:...) custom-call(f32[32,8960]{1,0:T(8,128)} %get-tuple-element.56.refs_0_, ...), custom_call_target="tpu_custom_call" | custom-call | tf_op jit(solution)/shard_map/update/pallas_call | solution.py:847
